TPU v7x, 32 devices: a whole 2x2x4 slice. The times are simulated.
32 devices in a mesh: cell: 2 (over x), ap: 8 (over z, y), sc: 2 (over core).
Axes of the slice: x: 2, y: 2, z: 4, core: 2. Of those that a mesh axis runs over, the one named last changes fastest.
Arguments:
- unsmoothed_link_guesses: bfloat16 [32, 4, 2, 128, 2048], P(('cell', 'ap'), None, None, None, 'sc'), parts along dimension 0, may hold values from -24 to 24
- received: bfloat16 [32, 4, 2, 4, 2048], P(('cell', 'ap'), None, None, None, 'sc'), parts along dimension 0, may hold values from -6 to 6
- user_power: float32 [256], P('cell'), parts along dimension 0, may hold values from 0.25 to 4
- noise_power: float32 [32], P(('cell', 'ap')), parts along dimension 0, may hold values from 0.1 to 1
- ap_gain: float32 [32, 128], P(('cell', 'ap')), parts along dimension 0, may hold values from 0.5 to 4
- user_cluster: int32 [256], P('cell'), parts along dimension 0, may hold values from 0 to 15, as said below
- serving: int32 [32, 16], P('cell'), parts along dimension 0, may hold values from 0 to 1, as said below
- cluster_owner: int32 [32, 1], P('cell'), parts along dimension 0, may hold values from 0 to 7, as said below
Outputs:
- estimates: float32 [64, 8, 4, 2, 2048], P(('cell', 'ap'), None, None, None, 'sc'), parts along dimension 0
There are 2 independent parts, one for each index of `cell`. A program takes and returns all parts, laid end to end along the dimension named above; each array names one. Nothing has to cross between parts.
Inputs may be any that keep to these rules, and one draw needn't show every extreme that they name: `user_cluster`: each of the 16 clusters holds exactly 8 users. `serving`: column a belongs to index a // 2 of ap. Where a cluster is served by an index of ap, at least one of its access points serves it. Of the clusters that one index of ap serves, at most 2 have the same owner; in every draw some owner has exactly 2 of its clusters served by every index of ap. `cluster_owner`: at most 4 clusters have the same owner, and some owner has exactly 4.
All inputs are finite; a program needn't handle non-finite values.
Results may differ from a plain program's by a relative error of at most 0.017.
Values may be sent and summed in bfloat16 or wider, within the bound.
A program may use at most 128 MiB of HBM per device.

v0:
```python
import functools
import math

import jax
import jax.numpy as jnp
import numpy as np
from jax import lax
from jax.experimental import pallas as pl
from jax.experimental.pallas import tpu as pltpu
from jax.sharding import PartitionSpec as P

TONE_NUMBER = 2048
TAPS = 64
CU = 8
OWN_MAX = 4
PEER_MAX = 2
MESH = pl.DeviceIdType.MESH
LANES = 128
VMEM_BYTES = 67043328


def complex_times(left_factor, right_factor):
    return (
        left_factor[0] * right_factor[0] - left_factor[1] * right_factor[1],
        left_factor[0] * right_factor[1] + left_factor[1] * right_factor[0],
    )


def times_conj(left_factor, right_factor):
    return (
        left_factor[0] * right_factor[0] + left_factor[1] * right_factor[1],
        left_factor[1] * right_factor[0] - left_factor[0] * right_factor[1],
    )


def hermitian_solve(cov_re, cov_im, right):
    dimension = len(cov_re)
    factor = {}
    inverses = []
    for j in range(dimension):
        pivot = cov_re[j][j]
        for k in range(j):
            element = factor[j, k]
            pivot = pivot - (element[0] * element[0] + element[1] * element[1])
        inverse = 1.0 / jnp.sqrt(pivot)
        inverses.append(inverse)
        for i in range(j + 1, dimension):
            running = (cov_re[i][j], cov_im[i][j])
            for k in range(j):
                product = times_conj(factor[i, k], factor[j, k])
                running = (running[0] - product[0], running[1] - product[1])
            factor[i, j] = (running[0] * inverse, running[1] * inverse)
    forward = []
    for i in range(dimension):
        running = right[i]
        for k in range(i):
            product = complex_times(factor[i, k], forward[k])
            running = (running[0] - product[0], running[1] - product[1])
        forward.append((running[0] * inverses[i], running[1] * inverses[i]))
    result = [None] * dimension
    for i in range(dimension - 1, -1, -1):
        running = forward[i]
        for k in range(i + 1, dimension):
            product = times_conj(result[k], factor[k, i])
            running = (running[0] - product[0], running[1] - product[1])
        result[i] = (running[0] * inverses[i], running[1] * inverses[i])
    return result


def delay_tables(parts, tones):
    made = []
    for part in range(parts):
        values = part * tones + np.arange(tones, dtype=np.int32)
        rotation = np.arange(TAPS, dtype=np.int32)[:, None] * values[None, :] % TONE_NUMBER
        angles = rotation.astype(np.float32) * np.float32(2.0 * math.pi / TONE_NUMBER)
        cosine, sine = np.cos(angles), np.sin(angles)
        made.append(
            np.concatenate(
                [
                    np.concatenate([cosine, sine], axis=0),
                    np.concatenate([-sine, cosine], axis=0),
                ],
                axis=1,
            )
        )
    return np.stack(made).astype(jnp.bfloat16)


def exact_dot(left, right, dims):
    return lax.dot_general(
        left.astype(jnp.bfloat16),
        right.astype(jnp.bfloat16),
        (dims, ((), ())),
        preferred_element_type=jnp.float32,
    )


def iota(shape, dim):
    return lax.broadcasted_iota(jnp.int32, shape, dim).astype(jnp.float32)


def user_tables(user_cluster, serving, owner, clusters, users, group, n):
    onehot = (iota((clusters, users), 0) == user_cluster.astype(jnp.float32)).astype(jnp.float32)
    owner_row = owner.astype(jnp.float32)
    square = (clusters, clusters)
    rows, cols = iota(square, 0), iota(square, 1)
    owner_col = jnp.sum(jnp.where(rows == cols, owner_row, 0.0), axis=1, keepdims=True)
    same = owner_col == owner_row
    earlier = jnp.where(same & (cols < rows), 1.0, 0.0)
    serve = serving.astype(jnp.float32)
    pair = jnp.where(
        jnp.floor((iota((group * n, n), 0) + 0.5) * (1.0 / group)) == iota((group * n, n), 1),
        1.0,
        0.0,
    )
    served = jnp.where(exact_dot(serve, pair, ((1,), (0,))) > 0.5, 1.0, 0.0)
    before = exact_dot(earlier, served, ((1,), (0,)))
    rank = jnp.sum(earlier, axis=1, keepdims=True)
    owner_u = jnp.sum(onehot * owner_col, axis=0, keepdims=True)
    rank_u = jnp.sum(onehot * rank, axis=0, keepdims=True)
    served_u = exact_dot(served, onehot, ((0,), (0,)))
    before_u = exact_dot(before, onehot, ((0,), (0,)))
    serve_u = exact_dot(serve, onehot, ((0,), (0,)))
    equal = exact_dot(onehot, onehot, ((0,), (0,)))
    both = (users, users)
    position = jnp.sum(
        jnp.where(iota(both, 0) < iota(both, 1), equal, 0.0), axis=0, keepdims=True
    )
    return owner_u, rank_u, served_u, before_u, serve_u, position


def first_kernel(
    n,
    chunks,
    ring_of,
    guess_hbm,
    received_hbm,
    power_hbm,
    noise_hbm,
    gain_hbm,
    cluster_hbm,
    serving_hbm,
    owner_hbm,
    table_hbm,
    share_ref,
    rank_ref,
    coef_all,
    solved_all,
    wrow_ref,
    received_ref,
    power_ref,
    noise_ref,
    gain_ref,
    cluster_ref,
    serving_ref,
    owner_ref,
    solved_wide,
    guess,
    table,
    half,
    other,
    coef_send,
    coef_b,
    gains,
    pick,
    power_wide,
    smooth,
    cov,
    own,
    guess_sem,
    table_sem,
    half_send_sem,
    half_recv_sem,
    gain_send_sem,
    gain_recv_sem,
    coef_send_sem,
    coef_recv_sem,
    ring_send_sem,
    ring_recv_sem,
    local_sem,
    small_sem,
    relay_send_sem,
    relay_recv_sem,
):
    stations, antennas, _, users, tones = guess.shape
    pieces = stations * antennas
    block = PEER_MAX * CU
    clusters = serving_ref.shape[0]
    me = lax.axis_index("ap")
    part = lax.axis_index("sc")
    node, place = ring_of
    spot = place(me)
    right = node(lax.rem(spot + 1, n))
    left = node(lax.rem(spot + n - 1, n))

    table_copy = pltpu.make_async_copy(table_hbm.at[part], table, table_sem)
    table_copy.start()
    small_copies = []
    for source, into in (
        (cluster_hbm, cluster_ref),
        (serving_hbm, serving_ref),
        (owner_hbm, owner_ref),
        (power_hbm, power_ref),
        (gain_hbm, gain_ref),
        (noise_hbm, noise_ref),
        (received_hbm, received_ref),
    ):
        copy = pltpu.make_async_copy(source, into, small_sem.at[len(small_copies)])
        copy.start()
        small_copies.append(copy)
    guess_copies = []
    for q in range(pieces):
        a, i = q // antennas, q % antennas
        copy = pltpu.make_async_copy(guess_hbm.at[a, i], guess.at[a, i], guess_sem.at[q])
        copy.start()
        guess_copies.append(copy)

    barrier = pltpu.get_barrier_semaphore()
    pl.semaphore_signal(barrier, inc=1, device_id={"sc": 1 - part}, device_id_type=MESH)
    for k in range(1, n):
        pl.semaphore_signal(
            barrier, inc=1, device_id={"ap": lax.rem(me + k, n)}, device_id_type=MESH
        )

    for copy in small_copies:
        copy.wait()
    owner_u, rank_u, served_u, before_u, serve_u, position = user_tables(
        cluster_ref[...], serving_ref[...], owner_ref[...], clusters, users, stations, n
    )
    mef = me.astype(jnp.float32)
    mine = iota((n, users), 0) == mef
    served_me = jnp.sum(jnp.where(mine, served_u, 0.0), axis=0, keepdims=True)
    before_me = jnp.sum(jnp.where(mine, before_u, 0.0), axis=0, keepdims=True)
    target = jnp.where(
        served_me > 0.5, owner_u * block + before_me * CU + position, -1.0
    )
    pick[...] = jnp.where(iota((n * block, users), 0) == target, 1.0, 0.0).astype(jnp.bfloat16)
    wide = jnp.broadcast_to(power_ref[...] * (1.0 / users), (LANES, users))
    power_wide[...] = jnp.transpose(wide)

    pl.semaphore_wait(barrier, n)

    gain_copies = []
    for k in range(1, n):
        peer = lax.rem(me + k, n)
        copy = pltpu.make_async_remote_copy(
            src_ref=gain_ref,
            dst_ref=gains.at[me],
            send_sem=gain_send_sem.at[k],
            recv_sem=gain_recv_sem.at[n - k],
            device_id={"ap": peer},
            device_id_type=MESH,
        )
        copy.start()
        gain_copies.append(copy)
    gains[me] = gain_ref[...]

    table_copy.wait()
    half_copies = []
    contract = (((1,), (1,)), ((), ()))
    for q in range(pieces):
        a, i = q // antennas, q % antennas
        guess_copies[q].wait()
        sums = lax.dot_general(
            guess[a, i, 0], table[:, :tones], contract, preferred_element_type=jnp.float32
        ) + lax.dot_general(
            guess[a, i, 1], table[:, tones:], contract, preferred_element_type=jnp.float32
        )
        half[q] = (sums * (1.0 / TONE_NUMBER)).astype(jnp.bfloat16)
        copy = pltpu.make_async_remote_copy(
            src_ref=half.at[q],
            dst_ref=other.at[q],
            send_sem=half_send_sem.at[q],
            recv_sem=half_recv_sem.at[q],
            device_id={"sc": 1 - part},
            device_id_type=MESH,
        )
        copy.start()
        half_copies.append(copy)
    for q in range(pieces):
        half_copies[q].wait_recv()
        total = (half[q].astype(jnp.float32) + other[q].astype(jnp.float32)).astype(jnp.bfloat16)
        coef_b[pl.ds(q * users, users), :] = total
        chosen = jnp.dot(pick[...], total, preferred_element_type=jnp.float32)
        coef_send[:, q] = chosen.astype(jnp.bfloat16).reshape(n, block, 2 * TAPS)
    coef_copies = []
    mine_half = pl.ds(part * (pieces // 2), pieces // 2)
    for k in range(1, n):
        peer = lax.rem(me + k, n)
        copy = pltpu.make_async_remote_copy(
            src_ref=coef_send.at[peer, mine_half],
            dst_ref=coef_all.at[me, mine_half],
            send_sem=coef_send_sem.at[k],
            recv_sem=coef_recv_sem.at[n - k],
            device_id={"ap": peer},
            device_id_type=MESH,
        )
        copy.start()
        coef_copies.append(copy)
    own_coef = pltpu.make_async_copy(coef_send.at[me], coef_all.at[me], local_sem)
    own_coef.start()

    width = tones // chunks
    symbols = received_ref.shape[3]
    rows = stations * symbols
    ring_copies = {}
    reach = {}
    for c in range(chunks):
        far, near = n // 2, n - 1 - n // 2
        reach[c] = (far, near) if c % 2 == 0 else (near, far)

    ready = []

    def origin_of(direction, step):
        back = lax.rem(spot + n - step, n) if direction == 0 else lax.rem(spot + step, n)
        return node(back)

    def ring_start(c, direction, step):
        if step > reach[c][direction]:
            return
        origin = origin_of(direction, step)
        source = own.at[c]
        if step > 0:
            ring_copies[c, direction, step - 1].wait_recv()
            source = solved_all.at[origin, c]
            ready.append((origin, c, source))
        if step == reach[c][direction]:
            return
        copy = pltpu.make_async_remote_copy(
            src_ref=source,
            dst_ref=solved_all.at[origin, c],
            send_sem=ring_send_sem.at[direction, c, step],
            recv_sem=ring_recv_sem.at[direction, c, step],
            device_id={"ap": right if direction == 0 else left},
            device_id_type=MESH,
        )
        copy.start()
        ring_copies[c, direction, step] = copy

    steps = max(max(r) for r in reach.values())
    entries = [(i, j) for i in range(antennas) for j in range(i + 1)]
    noise = jnp.concatenate(
        [
            jnp.broadcast_to(noise_ref[0:1, a : a + 1], (symbols, 1))
            for a in range(stations)
        ],
        axis=0,
    )
    for c in range(chunks):
        base = c * width
        for reim in range(2):
            columns = table[:, reim * tones + base : reim * tones + base + width]
            smooth[reim] = jnp.dot(coef_b[...], columns, preferred_element_type=jnp.float32)
        for a in range(stations):
            for l in range(width // LANES):
                lanes = pl.ds(l * LANES, LANES)

                def body(step, sums, a=a, lanes=lanes):
                    sums = list(sums)
                    for w in range(2):
                        row = (step * 2 + w) * 8
                        scale = power_wide[pl.ds(pl.multiple_of(row, 8), 8), :]
                        re, im = [], []
                        for i in range(antennas):
                            at = pl.multiple_of((a * antennas + i) * users + row, 8)
                            re.append(smooth[0, pl.ds(at, 8), lanes])
                            im.append(smooth[1, pl.ds(at, 8), lanes])
                        at = 0
                        for i in range(antennas):
                            sre, sim = re[i] * scale, im[i] * scale
                            for j in range(i + 1):
                                sums[at] = sums[at] + (sre * re[j] + sim * im[j])
                                at += 1
                                if j < i:
                                    sums[at] = sums[at] + (sim * re[j] - sre * im[j])
                                    at += 1
                    return tuple(sums)

                zero = jnp.zeros((8, LANES), jnp.float32)
                sums = lax.fori_loop(0, users // 16, body, (zero,) * (antennas * antennas))
                for e in range(antennas * antennas):
                    value = jnp.sum(sums[e], axis=0, keepdims=True)
                    cov[e, a * symbols : (a + 1) * symbols, lanes] = jnp.broadcast_to(
                        value, (symbols, LANES)
                    )
        cov_re = [[None] * antennas for _ in range(antennas)]
        cov_im = [[None] * antennas for _ in range(antennas)]
        at = 0
        for i, j in entries:
            cov_re[i][j] = cov[at]
            at += 1
            if i == j:
                cov_re[i][j] = cov_re[i][j] + noise
            else:
                cov_im[i][j] = cov[at]
                at += 1
        signal = []
        for i in range(antennas):
            signal.append(
                tuple(
                    jnp.concatenate(
                        [
                            received_ref[a, i, reim, :, base : base + width].astype(jnp.float32)
                            for a in range(stations)
                        ],
                        axis=0,
                    )
                    for reim in range(2)
                )
            )
        solved = hermitian_solve(cov_re, cov_im, signal)
        for i in range(antennas):
            joined = jnp.concatenate([solved[i][0], solved[i][1]], axis=0)
            own[c, pl.ds(i * 2 * rows, 2 * rows), :] = joined.astype(jnp.bfloat16)
        ready.append((me, c, own.at[c]))
        for d in range(c + 1):
            for direction in range(2):
                ring_start(d, direction, c - d)

    for copy in gain_copies:
        copy.wait_recv()
    weights = []
    totals = jnp.zeros((1, users), jnp.float32)
    for p in range(n):
        for a in range(stations):
            row = serve_u[p * stations + a : p * stations + a + 1] * gains[p, a : a + 1, :]
            weights.append(row)
            totals = totals + row
    scale = 1.0 / (1.0 + totals)
    for p in range(n):
        goal = jnp.where(
            (owner_u == mef) & (served_u[p : p + 1] > 0.5),
            before_u[p : p + 1] * CU + position,
            -1.0,
        )
        hits = iota((block, users), 0) == goal
        for a in range(stations):
            value = jnp.sum(
                jnp.where(hits, weights[p * stations + a] * scale, 0.0), axis=1, keepdims=True
            )
            wrow_ref[p, a] = jnp.broadcast_to(value, (block, LANES))
        for k in range(PEER_MAX):
            value = jnp.sum(
                jnp.where(hits[k * CU : k * CU + 1], rank_u, 0.0), axis=1, keepdims=True
            )
            rank_ref[p * PEER_MAX + k : p * PEER_MAX + k + 1, :] = jnp.broadcast_to(
                value, (1, LANES)
            ).astype(jnp.int32)


    relay_copies = []
    for k in range(1, n):
        coef_copies[n - k - 1].wait_recv()
        origin = lax.rem(me + n - (n - k), n)
        copy = pltpu.make_async_remote_copy(
            src_ref=coef_all.at[origin, mine_half],
            dst_ref=coef_all.at[origin, mine_half],
            send_sem=relay_send_sem.at[k],
            recv_sem=relay_recv_sem.at[k],
            device_id={"sc": 1 - part},
            device_id_type=MESH,
        )
        copy.start()
        relay_copies.append(copy)
    own_coef.wait()

    def combine(origin, c, source):
        base = c * width
        solved_wide[...] = source[...].astype(jnp.float32)
        coefs = coef_all[origin].reshape(pieces * block, 2 * TAPS)
        for reim in range(2):
            columns = table[:, reim * tones + base : reim * tones + base + width]
            smooth[reim, : pieces * block, :] = jnp.dot(
                coefs, columns, preferred_element_type=jnp.float32
            )

        def tile(l, carry):
            lanes = pl.ds(pl.multiple_of(l * LANES, LANES), LANES)
            sums = [[[None, None] for _ in range(symbols)] for _ in range(PEER_MAX)]
            for a in range(stations):
                weight = [wrow_ref[origin, a, pl.ds(k * CU, CU), :] for k in range(PEER_MAX)]
                for i in range(antennas):
                    re, im = [], []
                    for k in range(PEER_MAX):
                        at = (a * antennas + i) * block + k * CU
                        re.append(smooth[0, pl.ds(at, CU), lanes] * weight[k])
                        im.append(smooth[1, pl.ds(at, CU), lanes] * weight[k])
                    for s in range(symbols):
                        first = i * 2 * rows + a * symbols + s
                        sre = solved_wide[pl.ds(first, 1), lanes]
                        sim = solved_wide[pl.ds(first + rows, 1), lanes]
                        for k in range(PEER_MAX):
                            new_re = re[k] * sre + im[k] * sim
                            new_im = re[k] * sim - im[k] * sre
                            old = sums[k][s]
                            if old[0] is not None:
                                new_re, new_im = old[0] + new_re, old[1] + new_im
                            sums[k][s] = [new_re, new_im]
            for k in range(PEER_MAX):
                for s in range(symbols):
                    for reim in range(2):
                        share_ref[
                            c * (width // LANES) + l,
                            origin * PEER_MAX + k,
                            pl.ds((s * 2 + reim) * CU, CU),
                            :,
                        ] = sums[k][s][reim]
            return carry

        lax.fori_loop(0, width // LANES, tile, 0)

    def drain(most):
        for _ in range(most):
            if ready:
                combine(*ready.pop(0))

    late_slots = range(chunks, chunks + steps)
    for late in late_slots:
        for d in range(chunks):
            for direction in range(2):
                if late - d > 0:
                    ring_start(d, direction, late - d)
        if late == chunks:
            for copy in relay_copies:
                copy.wait_recv()
        drain(-(-n * chunks // (steps + 1)))
    drain(len(ready))
    for copy in relay_copies:
        copy.wait_send()
    for copy in half_copies:
        copy.wait_send()
    for copy in gain_copies:
        copy.wait_send()
    for copy in coef_copies:
        copy.wait_send()
    for copy in ring_copies.values():
        copy.wait_send()


def second_kernel(n, rank_ref, share_ref, out_hbm, total, moved, out_sem):
    tiles, _, rows, _ = share_ref.shape
    pairs = rows // (2 * CU)
    height = CU * pairs * tiles * 2
    total[...] = jnp.zeros_like(total)
    slots = [rank_ref[k, 0] for k in range(n * PEER_MAX)]

    def tile(l, carry):
        for k in range(n * PEER_MAX):
            total[l, slots[k]] += share_ref[l, k]
        return carry

    lax.fori_loop(0, tiles, tile, 0)
    copies = []
    for r in range(OWN_MAX):

        def move(l, carry, r=r):
            for s in range(pairs):
                for reim in range(2):
                    moved[pl.ds(r * height + (s * tiles + l) * 2 + reim, CU, stride=pairs * tiles * 2), :] = (
                        total[l, r, pl.ds((s * 2 + reim) * CU, CU), :]
                    )
            return carry

        lax.fori_loop(0, tiles, move, 0)
        part = pl.ds(r * height, height)
        copy = pltpu.make_async_copy(moved.at[part], out_hbm.at[part], out_sem.at[r])
        copy.start()
        copies.append(copy)
    for copy in copies:
        copy.wait()


def ring_functions(mesh):
    n = mesh.shape["ap"]
    half = n // 2

    def plain(q):
        return q

    def node(q):
        upper = q // half
        return (1 - upper) * 2 * q + upper * (2 * (n - q) - 1)

    def place(d):
        odd = d % 2
        return (1 - odd) * (d // 2) + odd * (n - (d + 1) // 2)

    if n % 2:
        return plain, plain
    try:
        axes = list(mesh.axis_names)
        line = np.moveaxis(mesh.devices, axes.index("ap"), 0).reshape(n, -1)[:, 0]
        spots = [tuple(d.coords) for d in line]
        sizes = [max(s[x] for s in spots) + 1 for x in range(3)]

        def length(order):
            far = 0
            for q in range(n):
                one, two = spots[order(q)], spots[order((q + 1) % n)]
                far += sum(
                    min(abs(one[x] - two[x]), sizes[x] - abs(one[x] - two[x])) for x in range(3)
                )
            return far

        if length(plain) < length(node):
            return plain, plain
    except (AttributeError, TypeError):
        pass
    return node, place


def local(
    n,
    parts,
    ring_of,
    unsmoothed_link_guesses,
    received,
    user_power,
    noise_power,
    ap_gain,
    user_cluster,
    serving,
    cluster_owner,
):
    stations, antennas, _, users, tones = unsmoothed_link_guesses.shape
    symbols = received.shape[3]
    pieces = stations * antennas
    block = PEER_MAX * CU
    rows = stations * symbols
    chunks = 2
    width = tones // chunks
    steps = n // 2
    table = jnp.asarray(delay_tables(parts, tones))
    vmem = pl.BlockSpec(memory_space=pltpu.VMEM)
    smem = pl.BlockSpec(memory_space=pltpu.SMEM)
    anywhere = pl.BlockSpec(memory_space=pl.ANY)
    dma = pltpu.SemaphoreType.DMA
    bf16, f32 = jnp.bfloat16, jnp.float32
    hbm = pl.BlockSpec(memory_space=pltpu.HBM)
    tiles = tones // LANES
    held = 4 * LANES * n * PEER_MAX * (tiles * symbols * 2 * CU + 1)
    share, rank = pl.pallas_call(
        functools.partial(first_kernel, n, chunks, ring_of),
        out_shape=(
            jax.ShapeDtypeStruct((tiles, n * PEER_MAX, symbols * 2 * CU, LANES), f32),
            jax.ShapeDtypeStruct((n * PEER_MAX, LANES), jnp.int32),
        ),
        in_specs=[hbm] * 9,
        out_specs=(vmem, vmem),
        scratch_shapes=[
            pltpu.VMEM((n, pieces, block, 2 * TAPS), bf16),
            pltpu.VMEM((n, chunks, antennas * 2 * rows, width), bf16),
            pltpu.VMEM((n, stations, block, LANES), f32),
            pltpu.VMEM(received.shape, bf16),
            pltpu.VMEM((1, users), f32),
            pltpu.VMEM((1, stations), f32),
            pltpu.VMEM((stations, users), f32),
            pltpu.VMEM((1, users), jnp.int32),
            pltpu.VMEM(serving.shape, jnp.int32),
            pltpu.VMEM((1, serving.shape[0]), jnp.int32),
            pltpu.VMEM((antennas * 2 * rows, width), f32),
            pltpu.VMEM((stations, antennas, 2, users, tones), bf16),
            pltpu.VMEM((2 * TAPS, 2 * tones), bf16),
            pltpu.VMEM((pieces, users, 2 * TAPS), bf16),
            pltpu.VMEM((pieces, users, 2 * TAPS), bf16),
            pltpu.VMEM((n, pieces, block, 2 * TAPS), bf16),
            pltpu.VMEM((pieces * users, 2 * TAPS), bf16),
            pltpu.VMEM((n, stations, users), f32),
            pltpu.VMEM((n * block, users), bf16),
            pltpu.VMEM((users, LANES), f32),
            pltpu.VMEM((2, pieces * users, width), f32),
            pltpu.VMEM((antennas * antennas, rows, width), f32),
            pltpu.VMEM((chunks, antennas * 2 * rows, width), bf16),
            dma((pieces,)),
            dma,
            dma((pieces,)),
            dma((pieces,)),
            dma((n,)),
            dma((n,)),
            dma((n,)),
            dma((n,)),
            dma((2, chunks, steps)),
            dma((2, chunks, steps)),
            dma,
            dma((7,)),
            dma((n,)),
            dma((n,)),
        ],
        compiler_params=pltpu.CompilerParams(
            collective_id=0, has_side_effects=True, vmem_limit_bytes=VMEM_BYTES - held
        ),
        name="smooth_solve_combine",
    )(
        unsmoothed_link_guesses,
        received,
        user_power.reshape(1, users),
        noise_power.reshape(1, stations),
        ap_gain,
        user_cluster.reshape(1, users),
        serving,
        cluster_owner.reshape(1, -1),
        table,
    )
    lines = OWN_MAX * CU * symbols * tiles * 2
    placed = pl.pallas_call(
        functools.partial(second_kernel, n),
        out_shape=jax.ShapeDtypeStruct((lines, LANES), f32),
        in_specs=[smem, vmem],
        out_specs=hbm,
        scratch_shapes=[
            pltpu.VMEM((tiles, OWN_MAX, symbols * 2 * CU, LANES), f32),
            pltpu.VMEM((lines, LANES), f32),
            dma((OWN_MAX,)),
        ],
        compiler_params=pltpu.CompilerParams(vmem_limit_bytes=16 * 1024 * 1024),
        name="place",
    )(rank, share)
    placed = placed.reshape(OWN_MAX, CU, symbols, tiles, 2, LANES)
    placed = jnp.transpose(placed, (0, 1, 2, 4, 3, 5))
    return placed.reshape(OWN_MAX, CU, symbols, 2, tones)


def solution(mesh):
    placed = (
        P(("cell", "ap"), None, None, None, "sc"),
        P(("cell", "ap"), None, None, None, "sc"),
        P("cell"),
        P(("cell", "ap")),
        P(("cell", "ap"), None),
        P("cell"),
        P("cell", None),
        P("cell", None),
    )
    return jax.shard_map(
        functools.partial(local, mesh.shape["ap"], mesh.shape["sc"], ring_functions(mesh)),
        mesh=mesh,
        in_specs=placed,
        out_specs=P(("cell", "ap"), None, None, None, "sc"),
        check_vma=False,
    )
```

profile of v0, /device:TPU:0, one launch (start us, length us, event | category | flops | bytes accessed | tf_op | source)
XLA Modules:
  0.0 44.1 jit_solution(7076269038939458767)
XLA Ops:
  0.0 38.1 %smooth_solve_combine.1 = (f32[8,16,64,128]{3,2,1,0:T(8,128)}, s32[16,128]{1,0:T(8,128)}) custom-call(bf16[2,4,2,128,1024]{4,3,2,1,0:T(8,128)(2,1)} %guess_hbm.1, bf16[2,4,2,4,1024]{4,3,2,1,0:T(4,128)(2,1)} %received_hbm.1, f32[1,128]{1,0:T(1,128)} %bitcast.9, f32[1,2]{1,0:T(1,128)} %bitcast.10, f32[2,128]{1,0:T(2,128)} %gain_hbm.1, s32[1,128]{1,0:T(1,128)} %bitcast.11, ...), custom_call_target="tpu_custom_call" | custom-call | tf_op jit(solution)/shard_map/smooth_solve_combine/pallas_call | solution.py:642
  38.1 0.0 copy-start
  38.1 2.2 %copy-done = f32[8,16,64,128]{3,2,1,0:T(8,128)S(1)} copy-done((f32[8,16,64,128]{3,2,1,0:T(8,128)S(1)}, f32[8,16,64,128]{3,2,1,0:T(8,128)}, u32[]{:S(2)}) %copy-start) | copy-done | bytes 4194328
  40.3 0.0 copy-start.1
  40.3 0.7 %copy-done.1 = s32[16,128]{1,0:T(8,128)S(1)} copy-done((s32[16,128]{1,0:T(8,128)S(1)}, s32[16,128]{1,0:T(8,128)}, u32[]{:S(2)}) %copy-start.1) | copy-done | bytes 8216
  41.0 3.1 %place.1 = f32[2048,128]{1,0:T(8,128)} custom-call(s32[16,128]{1,0:T(8,128)S(1)} %copy-done.1, f32[8,16,64,128]{3,2,1,0:T(8,128)S(1)} %copy-done), custom_call_target="tpu_custom_call" | custom-call | tf_op jit(solution)/shard_map/place/pallas_call | solution.py:705
Async XLA Ops:
  38.1 2.2 %copy-start = (f32[8,16,64,128]{3,2,1,0:T(8,128)S(1)}, f32[8,16,64,128]{3,2,1,0:T(8,128)}, u32[]{:S(2)}) copy-start(f32[8,16,64,128]{3,2,1,0:T(8,128)} %get-tuple-element.8.share_ref) | copy-start | bytes 12582916
  40.3 0.7 %copy-start.1 = (s32[16,128]{1,0:T(8,128)S(1)}, s32[16,128]{1,0:T(8,128)}, u32[]{:S(2)}) copy-start(s32[16,128]{1,0:T(8,128)} %get-tuple-element.7.rank_ref) | copy-start | bytes 24580
where the time goes:
time: 44.3 us; the launch traced here: 44.1 us
  Pallas kernels  41.2 us (93%)
  local copies, waits for them, and re-layouts  2.88 us (7%)
    pallas_call x1, Pallas kernels, local(): pl.pallas_call(functools.partial(first_kernel, n, chunks, ring_of), out_s...  38.1 us
    pallas_call x1, Pallas kernels, local(): pl.pallas_call(functools.partial(second_kernel, n), out_shape=jax.ShapeDt...  3.14 us
    unnamed x4, local copies, waits for them, and re-layouts  2.88 us

commit v1 on v0

v1 whole, which is shorter than its diff:
```python
import functools
import math

import jax
import jax.numpy as jnp
import numpy as np
from jax import lax
from jax.experimental import pallas as pl
from jax.experimental.pallas import tpu as pltpu
from jax.sharding import PartitionSpec as P

TONE_NUMBER = 2048
TAPS = 64
CU = 8
OWN_MAX = 4
PEER_MAX = 2
COARSE = 2 * TAPS
MESH = pl.DeviceIdType.MESH
LANES = 128
VMEM_BYTES = 67043328


def complex_times(left_factor, right_factor):
    return (
        left_factor[0] * right_factor[0] - left_factor[1] * right_factor[1],
        left_factor[0] * right_factor[1] + left_factor[1] * right_factor[0],
    )


def times_conj(left_factor, right_factor):
    return (
        left_factor[0] * right_factor[0] + left_factor[1] * right_factor[1],
        left_factor[1] * right_factor[0] - left_factor[0] * right_factor[1],
    )


def hermitian_solve(cov_re, cov_im, right):
    dimension = len(cov_re)
    factor = {}
    inverses = []
    for j in range(dimension):
        pivot = cov_re[j][j]
        for k in range(j):
            element = factor[j, k]
            pivot = pivot - (element[0] * element[0] + element[1] * element[1])
        inverse = 1.0 / jnp.sqrt(pivot)
        inverses.append(inverse)
        for i in range(j + 1, dimension):
            running = (cov_re[i][j], cov_im[i][j])
            for k in range(j):
                product = times_conj(factor[i, k], factor[j, k])
                running = (running[0] - product[0], running[1] - product[1])
            factor[i, j] = (running[0] * inverse, running[1] * inverse)
    forward = []
    for i in range(dimension):
        running = right[i]
        for k in range(i):
            product = complex_times(factor[i, k], forward[k])
            running = (running[0] - product[0], running[1] - product[1])
        forward.append((running[0] * inverses[i], running[1] * inverses[i]))
    result = [None] * dimension
    for i in range(dimension - 1, -1, -1):
        running = forward[i]
        for k in range(i + 1, dimension):
            product = times_conj(result[k], factor[k, i])
            running = (running[0] - product[0], running[1] - product[1])
        result[i] = (running[0] * inverses[i], running[1] * inverses[i])
    return result


def angles_of(values):
    rotation = np.arange(TAPS, dtype=np.int32)[:, None] * values[None, :] % TONE_NUMBER
    return rotation.astype(np.float32) * np.float32(2.0 * math.pi / TONE_NUMBER)


def wave_table(values):
    cosine, sine = np.cos(angles_of(values)), np.sin(angles_of(values))
    return np.concatenate([cosine, sine], axis=0), np.concatenate([-sine, cosine], axis=0)


def tap_tables(parts, tones):
    made = []
    for part in range(parts):
        real, imag = wave_table(part * tones + np.arange(tones, dtype=np.int32))
        made.append(np.concatenate([real.T, imag.T], axis=0))
    return np.stack(made).astype(jnp.bfloat16)


def tone_tables(parts, tones):
    made = []
    for part in range(parts):
        real, imag = wave_table(part * tones + np.arange(tones, dtype=np.int32))
        pair = np.stack(
            [real.reshape(2 * TAPS, -1, LANES), imag.reshape(2 * TAPS, -1, LANES)], axis=2
        )
        made.append(pair.reshape(2 * TAPS, 2 * tones))
    return np.stack(made).astype(jnp.bfloat16)


def coarse_table():
    step = TONE_NUMBER // COARSE
    real, imag = wave_table(step * np.arange(COARSE, dtype=np.int32))
    return np.concatenate([real, imag], axis=1).astype(jnp.bfloat16)


def spread_tables(parts, tones):
    step = TONE_NUMBER // COARSE
    made = []
    for part in range(parts):
        values = part * tones + np.arange(tones, dtype=np.int64)
        gap = values[None, :] - step * np.arange(COARSE, dtype=np.int64)[:, None]
        kernel = np.ones(gap.shape, np.float64)
        for d in range(1, COARSE // 2 + 1):
            share = 2.0 if d < COARSE // 2 else 1.0
            kernel += share * np.cos(2.0 * math.pi / TONE_NUMBER * (d * gap % TONE_NUMBER))
        kernel /= COARSE
        high = kernel.astype(np.float32).astype(jnp.bfloat16)
        low = (kernel - high.astype(np.float64)).astype(np.float32).astype(jnp.bfloat16)
        made.append(np.concatenate([high, low], axis=0))
    return np.stack(made)


def exact_dot(left, right, dims):
    return lax.dot_general(
        left.astype(jnp.bfloat16),
        right.astype(jnp.bfloat16),
        (dims, ((), ())),
        preferred_element_type=jnp.float32,
    )


def iota(shape, dim):
    return lax.broadcasted_iota(jnp.int32, shape, dim).astype(jnp.float32)


def user_tables(user_cluster, serving, owner, clusters, users, group, n):
    onehot = (iota((clusters, users), 0) == user_cluster.astype(jnp.float32)).astype(jnp.float32)
    owner_row = owner.astype(jnp.float32)
    square = (clusters, clusters)
    rows, cols = iota(square, 0), iota(square, 1)
    owner_col = jnp.sum(jnp.where(rows == cols, owner_row, 0.0), axis=1, keepdims=True)
    same = owner_col == owner_row
    earlier = jnp.where(same & (cols < rows), 1.0, 0.0)
    serve = serving.astype(jnp.float32)
    pair = jnp.where(
        jnp.floor((iota((group * n, n), 0) + 0.5) * (1.0 / group)) == iota((group * n, n), 1),
        1.0,
        0.0,
    )
    served = jnp.where(exact_dot(serve, pair, ((1,), (0,))) > 0.5, 1.0, 0.0)
    before = exact_dot(earlier, served, ((1,), (0,)))
    rank = jnp.sum(earlier, axis=1, keepdims=True)
    owner_u = jnp.sum(onehot * owner_col, axis=0, keepdims=True)
    rank_u = jnp.sum(onehot * rank, axis=0, keepdims=True)
    served_u = exact_dot(served, onehot, ((0,), (0,)))
    before_u = exact_dot(before, onehot, ((0,), (0,)))
    serve_u = exact_dot(serve, onehot, ((0,), (0,)))
    equal = exact_dot(onehot, onehot, ((0,), (0,)))
    both = (users, users)
    position = jnp.sum(
        jnp.where(iota(both, 0) < iota(both, 1), equal, 0.0), axis=0, keepdims=True
    )
    return owner_u, rank_u, served_u, before_u, serve_u, position


def uplink_kernel(
    n,
    chunks,
    ring_of,
    guess_hbm,
    received_hbm,
    power_hbm,
    noise_hbm,
    gain_hbm,
    cluster_hbm,
    serving_hbm,
    owner_hbm,
    taps_hbm,
    table_hbm,
    coarse_hbm,
    spread_hbm,
    out_ref,
    coef_all,
    solved_all,
    received_ref,
    power_ref,
    noise_ref,
    gain_ref,
    cluster_ref,
    serving_ref,
    owner_ref,
    solved_wide,
    guess,
    taps,
    table,
    coarse,
    spread,
    half,
    other,
    coef_send,
    coef_b,
    gains,
    pick,
    pick_weight,
    power_wide,
    sampled,
    samples,
    cov,
    smooth,
    own,
    share,
    guess_sem,
    table_sem,
    half_send_sem,
    half_recv_sem,
    gain_send_sem,
    gain_recv_sem,
    coef_send_sem,
    coef_recv_sem,
    ring_send_sem,
    ring_recv_sem,
    local_sem,
    small_sem,
    relay_send_sem,
    relay_recv_sem,
):
    stations, antennas, _, users, tones = guess.shape
    pieces = stations * antennas
    block = PEER_MAX * CU
    clusters = serving_ref.shape[0]
    me = lax.axis_index("ap")
    part = lax.axis_index("sc")
    node, place = ring_of
    spot = place(me)
    right = node(lax.rem(spot + 1, n))
    left = node(lax.rem(spot + n - 1, n))

    table_copies = []
    for source, into in (
        (taps_hbm.at[part], taps),
        (coarse_hbm, coarse),
        (spread_hbm.at[part], spread),
        (table_hbm.at[part], table),
    ):
        table_copies.append(
            pltpu.make_async_copy(source, into, table_sem.at[len(table_copies)])
        )
    table_copies[0].start()
    guess_copies = []
    for q in range(pieces):
        a, i = q // antennas, q % antennas
        copy = pltpu.make_async_copy(guess_hbm.at[a, i], guess.at[a, i], guess_sem.at[q])
        copy.start()
        guess_copies.append(copy)
    small_copies = []
    for source, into in (
        (cluster_hbm, cluster_ref),
        (serving_hbm, serving_ref),
        (owner_hbm, owner_ref),
        (power_hbm, power_ref),
        (gain_hbm, gain_ref),
        (noise_hbm, noise_ref),
        (received_hbm, received_ref),
    ):
        copy = pltpu.make_async_copy(source, into, small_sem.at[len(small_copies)])
        copy.start()
        small_copies.append(copy)
    for copy in table_copies[1:]:
        copy.start()

    barrier = pltpu.get_barrier_semaphore()
    pl.semaphore_signal(barrier, inc=1, device_id={"sc": 1 - part}, device_id_type=MESH)
    for k in range(1, n):
        pl.semaphore_signal(
            barrier, inc=1, device_id={"ap": lax.rem(me + k, n)}, device_id_type=MESH
        )

    table_copies[0].wait()
    half_copies = []
    for q in range(pieces):
        a, i = q // antennas, q % antennas
        guess_copies[q].wait()
        sums = jnp.dot(
            guess[a, i, 0], taps[:tones, :], preferred_element_type=jnp.float32
        ) + jnp.dot(guess[a, i, 1], taps[tones:, :], preferred_element_type=jnp.float32)
        half[q] = (sums * (1.0 / TONE_NUMBER)).astype(jnp.bfloat16)
        if q == 0:
            pl.semaphore_wait(barrier, n)
        copy = pltpu.make_async_remote_copy(
            src_ref=half.at[q],
            dst_ref=other.at[q],
            send_sem=half_send_sem.at[q],
            recv_sem=half_recv_sem.at[q],
            device_id={"sc": 1 - part},
            device_id_type=MESH,
        )
        copy.start()
        half_copies.append(copy)

    for copy in small_copies:
        copy.wait()
    gain_copies = []
    for k in range(1, n):
        peer = lax.rem(me + k, n)
        copy = pltpu.make_async_remote_copy(
            src_ref=gain_ref,
            dst_ref=gains.at[me],
            send_sem=gain_send_sem.at[k],
            recv_sem=gain_recv_sem.at[n - k],
            device_id={"ap": peer},
            device_id_type=MESH,
        )
        copy.start()
        gain_copies.append(copy)
    gains[me] = gain_ref[...]
    owner_u, rank_u, served_u, before_u, serve_u, position = user_tables(
        cluster_ref[...], serving_ref[...], owner_ref[...], clusters, users, stations, n
    )
    mef = me.astype(jnp.float32)
    mine = iota((n, users), 0) == mef
    served_me = jnp.sum(jnp.where(mine, served_u, 0.0), axis=0, keepdims=True)
    before_me = jnp.sum(jnp.where(mine, before_u, 0.0), axis=0, keepdims=True)
    target = jnp.where(
        served_me > 0.5, owner_u * block + before_me * CU + position, -1.0
    )
    chosen_user = iota((n * block, users), 0) == target
    pick[...] = jnp.where(chosen_user, 1.0, 0.0).astype(jnp.bfloat16)
    for a in range(stations):
        row_here = iota((n * stations, users), 0) == mef * stations + a
        weight = jnp.sum(jnp.where(row_here, serve_u, 0.0), axis=0, keepdims=True)
        weight = weight * gain_ref[a : a + 1, :]
        column = jnp.sum(jnp.where(chosen_user, weight, 0.0), axis=1, keepdims=True)
        pick_weight[a] = jnp.broadcast_to(column, (n * block, LANES))
    wide = jnp.broadcast_to(power_ref[...] * (1.0 / users), (LANES, users))
    power_wide[...] = jnp.transpose(wide)

    for q in range(pieces):
        half_copies[q].wait_recv()
        total = (half[q].astype(jnp.float32) + other[q].astype(jnp.float32)).astype(jnp.bfloat16)
        coef_b[pl.ds(q * users, users), :] = total
        chosen = jnp.dot(pick[...], total, preferred_element_type=jnp.float32)
        chosen = chosen * pick_weight[q // antennas]
        coef_send[:, q] = chosen.astype(jnp.bfloat16).reshape(n, block, 2 * TAPS)
    coef_copies = []
    mine_half = pl.ds(part * (pieces // 2), pieces // 2)
    for k in range(1, n):
        peer = lax.rem(me + k, n)
        copy = pltpu.make_async_remote_copy(
            src_ref=coef_send.at[peer, mine_half],
            dst_ref=coef_all.at[me, mine_half],
            send_sem=coef_send_sem.at[k],
            recv_sem=coef_recv_sem.at[n - k],
            device_id={"ap": peer},
            device_id_type=MESH,
        )
        copy.start()
        coef_copies.append(copy)
    own_coef = pltpu.make_async_copy(coef_send.at[me], coef_all.at[me], local_sem)
    own_coef.start()

    width = tones // chunks
    lane_tiles = width // LANES
    symbols = received_ref.shape[3]
    rows = stations * symbols
    ring_copies = {}
    reach = {}
    for c in range(chunks):
        far, near = n // 2, n - 1 - n // 2
        reach[c] = (far, near) if c % 2 == 0 else (near, far)

    ready = []

    def origin_of(direction, step):
        back = lax.rem(spot + n - step, n) if direction == 0 else lax.rem(spot + step, n)
        return node(back)

    def ring_start(c, direction, step):
        if step > reach[c][direction]:
            return False
        origin = origin_of(direction, step)
        source = own.at[c]
        if step > 0:
            ring_copies[c, direction, step - 1].wait_recv()
            source = solved_all.at[origin, c]
            ready.append((origin, c, source))
        if step == reach[c][direction]:
            return True
        copy = pltpu.make_async_remote_copy(
            src_ref=source,
            dst_ref=solved_all.at[origin, c],
            send_sem=ring_send_sem.at[direction, c, step],
            recv_sem=ring_recv_sem.at[direction, c, step],
            device_id={"ap": right if direction == 0 else left},
            device_id_type=MESH,
        )
        copy.start()
        ring_copies[c, direction, step] = copy
        return True

    steps = max(max(r) for r in reach.values())
    entries = [(i, j) for i in range(antennas) for j in range(i + 1)]
    noise = jnp.concatenate(
        [
            jnp.broadcast_to(noise_ref[0:1, a : a + 1], (symbols, 1))
            for a in range(stations)
        ],
        axis=0,
    )

    for copy in table_copies[1:]:
        copy.wait()
    both = jnp.dot(coef_b[...], coarse[...], preferred_element_type=jnp.float32)
    for reim in range(2):
        sampled[reim] = both[:, reim * COARSE : (reim + 1) * COARSE]
    for a in range(stations):

        def body(step, sums, a=a):
            sums = list(sums)
            for w in range(2):
                row = (step * 2 + w) * 8
                scale = power_wide[pl.ds(pl.multiple_of(row, 8), 8), :]
                re, im = [], []
                for i in range(antennas):
                    at = pl.multiple_of((a * antennas + i) * users + row, 8)
                    re.append(sampled[0, pl.ds(at, 8), :])
                    im.append(sampled[1, pl.ds(at, 8), :])
                at = 0
                for i in range(antennas):
                    sre, sim = re[i] * scale, im[i] * scale
                    for j in range(i + 1):
                        sums[at] = sums[at] + (sre * re[j] + sim * im[j])
                        at += 1
                        if j < i:
                            sums[at] = sums[at] + (sim * re[j] - sre * im[j])
                            at += 1
            return tuple(sums)

        zero = jnp.zeros((8, COARSE), jnp.float32)
        sums = lax.fori_loop(0, users // 16, body, (zero,) * (antennas * antennas))
        for e in range(antennas * antennas):
            value = jnp.sum(sums[e], axis=0, keepdims=True)
            samples[pl.ds(e * rows + a * symbols, symbols), :] = jnp.broadcast_to(
                value, (symbols, COARSE)
            )
    high = samples[...].astype(jnp.bfloat16)
    low = (samples[...] - high.astype(jnp.float32)).astype(jnp.bfloat16)
    cov[...] = (
        jnp.dot(
            jnp.concatenate([high, high], axis=1),
            spread[...],
            preferred_element_type=jnp.float32,
        )
        + jnp.dot(low, spread[:COARSE, :], preferred_element_type=jnp.float32)
    )
    for c in range(chunks):
        base = c * width
        lanes = slice(base, base + width)
        cov_re = [[None] * antennas for _ in range(antennas)]
        cov_im = [[None] * antennas for _ in range(antennas)]
        at = 0
        for i, j in entries:
            cov_re[i][j] = cov[at * rows : (at + 1) * rows, lanes]
            at += 1
            if i == j:
                cov_re[i][j] = cov_re[i][j] + noise
            else:
                cov_im[i][j] = cov[at * rows : (at + 1) * rows, lanes]
                at += 1
        signal = []
        for i in range(antennas):
            signal.append(
                tuple(
                    jnp.concatenate(
                        [
                            received_ref[a, i, reim, :, lanes].astype(jnp.float32)
                            for a in range(stations)
                        ],
                        axis=0,
                    )
                    for reim in range(2)
                )
            )
        solved = hermitian_solve(cov_re, cov_im, signal)
        for i in range(antennas):
            joined = jnp.concatenate([solved[i][0], solved[i][1]], axis=0)
            own[c, pl.ds(i * 2 * rows, 2 * rows), :] = joined.astype(jnp.bfloat16)
        ready.append((me, c, own.at[c]))
        for d in range(c + 1):
            for direction in range(2):
                ring_start(d, direction, c - d)

    for copy in gain_copies:
        copy.wait_recv()
    totals = jnp.zeros((1, users), jnp.float32)
    for p in range(n):
        for a in range(stations):
            row = serve_u[p * stations + a : p * stations + a + 1] * gains[p, a : a + 1, :]
            totals = totals + row
    scale = 1.0 / (1.0 + totals)
    held = owner_u == mef
    slot_user = iota((OWN_MAX * CU, users), 0) == jnp.where(held, rank_u * CU + position, -1.0)
    slot_rows = jnp.where(slot_user, 1.0, 0.0)
    slot_scale = jnp.sum(jnp.where(slot_user, scale, 0.0), axis=1, keepdims=True)
    slot_scale = jnp.broadcast_to(slot_scale, (OWN_MAX * CU, LANES))
    hits = []
    for p in range(n):
        goal = jnp.where(
            held & (served_u[p : p + 1] > 0.5), before_u[p : p + 1] * CU + position, -1.0
        )
        hits.append(jnp.where(iota((block, users), 0) == goal, 1.0, 0.0))
    placement = exact_dot(slot_rows, jnp.concatenate(hits, axis=0), ((1,), (1,)))
    placement = placement.astype(jnp.bfloat16)

    relay_copies = []
    for k in range(1, n):
        coef_copies[n - k - 1].wait_recv()
        origin = lax.rem(me + n - (n - k), n)
        copy = pltpu.make_async_remote_copy(
            src_ref=coef_all.at[origin, mine_half],
            dst_ref=coef_all.at[origin, mine_half],
            send_sem=relay_send_sem.at[k],
            recv_sem=relay_recv_sem.at[k],
            device_id={"sc": 1 - part},
            device_id_type=MESH,
        )
        copy.start()
        relay_copies.append(copy)
    own_coef.wait()

    def combine(origin, c, source):
        wide = source[...].astype(jnp.float32)
        for i in range(antennas):
            re = wide[i * 2 * rows : i * 2 * rows + rows]
            im = wide[i * 2 * rows + rows : (i + 1) * 2 * rows]
            solved_wide[i, 0] = re
            solved_wide[i, 1] = im
            solved_wide[i, 2] = re + im
        coefs = coef_all[origin].reshape(pieces * block, 2 * TAPS)
        for l in range(lane_tiles):
            columns = pl.ds((c * lane_tiles + l) * 2 * LANES, 2 * LANES)
            smooth[l] = jnp.dot(coefs, table[:, columns], preferred_element_type=jnp.float32)
        for l in range(lane_tiles):
            lanes = pl.ds(l * LANES, LANES)
            sums = [[None] * symbols for _ in range(PEER_MAX)]
            for a in range(stations):
                for i in range(antennas):
                    re, im, gap = [], [], []
                    for k in range(PEER_MAX):
                        at = (a * antennas + i) * block + k * CU
                        re.append(smooth[l, pl.ds(at, CU), :LANES])
                        im.append(smooth[l, pl.ds(at, CU), LANES:])
                        gap.append(re[k] - im[k])
                    for s in range(symbols):
                        row = pl.ds(a * symbols + s, 1)
                        sre = solved_wide[i, 0, row, lanes]
                        sim = solved_wide[i, 1, row, lanes]
                        ssum = solved_wide[i, 2, row, lanes]
                        for k in range(PEER_MAX):
                            new = (re[k] * sre, im[k] * sim, gap[k] * ssum)
                            old = sums[k][s]
                            if old is not None:
                                new = tuple(x + y for x, y in zip(old, new))
                            sums[k][s] = new
            at = pl.ds(pl.multiple_of(origin * block, block), block)
            for s in range(symbols):
                first = [sums[k][s][0] + sums[k][s][1] for k in range(PEER_MAX)]
                second = [
                    sums[k][s][2] - (sums[k][s][0] - sums[k][s][1]) for k in range(PEER_MAX)
                ]
                for reim, values in ((0, first), (1, second)):
                    share[s * 2 + reim, at, pl.ds(c * width + l * LANES, LANES)] = (
                        jnp.concatenate(values, axis=0).astype(jnp.bfloat16)
                    )

    def drain(most):
        for _ in range(most):
            if ready:
                combine(*ready.pop(0))

    drain(1)
    waited = False
    for late in range(chunks, chunks + steps):
        for d in range(chunks):
            for direction in range(2):
                if late - d > 0 and ring_start(d, direction, late - d):
                    if not waited and len(ready) and ready[0][0] is not me:
                        for copy in relay_copies:
                            copy.wait_recv()
                        waited = True
                    drain(1)
    if not waited:
        for copy in relay_copies:
            copy.wait_recv()
    drain(len(ready))

    tiles = tones // LANES
    for s in range(symbols):
        for reim in range(2):
            placed = jnp.dot(placement, share[s * 2 + reim], preferred_element_type=jnp.float32)
            for l in range(tiles):
                for r in range(OWN_MAX):
                    value = placed[r * CU : (r + 1) * CU, l * LANES : (l + 1) * LANES]
                    first = r * CU * symbols * tiles * 2 + (s * tiles + l) * 2 + reim
                    out_ref[pl.ds(first, CU, stride=symbols * tiles * 2), :] = (
                        value * slot_scale[r * CU : (r + 1) * CU]
                    )

    for copy in relay_copies:
        copy.wait_send()
    for copy in half_copies:
        copy.wait_send()
    for copy in gain_copies:
        copy.wait_send()
    for copy in coef_copies:
        copy.wait_send()
    for copy in ring_copies.values():
        copy.wait_send()


def ring_functions(mesh):
    n = mesh.shape["ap"]
    half = n // 2

    def plain(q):
        return q

    def node(q):
        upper = q // half
        return (1 - upper) * 2 * q + upper * (2 * (n - q) - 1)

    def place(d):
        odd = d % 2
        return (1 - odd) * (d // 2) + odd * (n - (d + 1) // 2)

    if n % 2:
        return plain, plain
    try:
        axes = list(mesh.axis_names)
        line = np.moveaxis(mesh.devices, axes.index("ap"), 0).reshape(n, -1)[:, 0]
        spots = [tuple(d.coords) for d in line]
        sizes = [max(s[x] for s in spots) + 1 for x in range(3)]

        def length(order):
            far = 0
            for q in range(n):
                one, two = spots[order(q)], spots[order((q + 1) % n)]
                far += sum(
                    min(abs(one[x] - two[x]), sizes[x] - abs(one[x] - two[x])) for x in range(3)
                )
            return far

        if length(plain) < length(node):
            return plain, plain
    except (AttributeError, TypeError):
        pass
    return node, place


def local(
    n,
    parts,
    ring_of,
    unsmoothed_link_guesses,
    received,
    user_power,
    noise_power,
    ap_gain,
    user_cluster,
    serving,
    cluster_owner,
):
    stations, antennas, _, users, tones = unsmoothed_link_guesses.shape
    symbols = received.shape[3]
    pieces = stations * antennas
    block = PEER_MAX * CU
    rows = stations * symbols
    chunks = 2
    width = tones // chunks
    steps = n // 2
    vmem = pl.BlockSpec(memory_space=pltpu.VMEM)
    dma = pltpu.SemaphoreType.DMA
    bf16, f32 = jnp.bfloat16, jnp.float32
    hbm = pl.BlockSpec(memory_space=pltpu.HBM)
    tiles = tones // LANES
    lines = OWN_MAX * CU * symbols * tiles * 2
    placed = pl.pallas_call(
        functools.partial(uplink_kernel, n, chunks, ring_of),
        out_shape=jax.ShapeDtypeStruct((lines, LANES), f32),
        in_specs=[hbm] * 12,
        out_specs=vmem,
        scratch_shapes=[
            pltpu.VMEM((n, pieces, block, 2 * TAPS), bf16),
            pltpu.VMEM((n, chunks, antennas * 2 * rows, width), bf16),
            pltpu.VMEM(received.shape, bf16),
            pltpu.VMEM((1, users), f32),
            pltpu.VMEM((1, stations), f32),
            pltpu.VMEM((stations, users), f32),
            pltpu.VMEM((1, users), jnp.int32),
            pltpu.VMEM(serving.shape, jnp.int32),
            pltpu.VMEM((1, serving.shape[0]), jnp.int32),
            pltpu.VMEM((antennas, 3, rows, width), f32),
            pltpu.VMEM((stations, antennas, 2, users, tones), bf16),
            pltpu.VMEM((2 * tones, 2 * TAPS), bf16),
            pltpu.VMEM((2 * TAPS, 2 * tones), bf16),
            pltpu.VMEM((2 * TAPS, 2 * COARSE), bf16),
            pltpu.VMEM((2 * COARSE, tones), bf16),
            pltpu.VMEM((pieces, users, 2 * TAPS), bf16),
            pltpu.VMEM((pieces, users, 2 * TAPS), bf16),
            pltpu.VMEM((n, pieces, block, 2 * TAPS), bf16),
            pltpu.VMEM((pieces * users, 2 * TAPS), bf16),
            pltpu.VMEM((n, stations, users), f32),
            pltpu.VMEM((n * block, users), bf16),
            pltpu.VMEM((stations, n * block, LANES), f32),
            pltpu.VMEM((users, LANES), f32),
            pltpu.VMEM((2, pieces * users, COARSE), f32),
            pltpu.VMEM((antennas * antennas * rows, COARSE), f32),
            pltpu.VMEM((antennas * antennas * rows, tones), f32),
            pltpu.VMEM((width // LANES, pieces * block, 2 * LANES), f32),
            pltpu.VMEM((chunks, antennas * 2 * rows, width), bf16),
            pltpu.VMEM((symbols * 2, n * block, tones), bf16),
            dma((pieces,)),
            dma((4,)),
            dma((pieces,)),
            dma((pieces,)),
            dma((n,)),
            dma((n,)),
            dma((n,)),
            dma((n,)),
            dma((2, chunks, steps)),
            dma((2, chunks, steps)),
            dma,
            dma((7,)),
            dma((n,)),
            dma((n,)),
        ],
        compiler_params=pltpu.CompilerParams(
            collective_id=0, has_side_effects=True, vmem_limit_bytes=VMEM_BYTES
        ),
        name="uplink",
    )(
        unsmoothed_link_guesses,
        received,
        user_power.reshape(1, users),
        noise_power.reshape(1, stations),
        ap_gain,
        user_cluster.reshape(1, users),
        serving,
        cluster_owner.reshape(1, -1),
        jnp.asarray(tap_tables(parts, tones)),
        jnp.asarray(tone_tables(parts, tones)),
        jnp.asarray(coarse_table()),
        jnp.asarray(spread_tables(parts, tones)),
    )
    placed = placed.reshape(OWN_MAX, CU, symbols, tiles, 2, LANES)
    placed = jnp.transpose(placed, (0, 1, 2, 4, 3, 5))
    return placed.reshape(OWN_MAX, CU, symbols, 2, tones)


def solution(mesh):
    placed = (
        P(("cell", "ap"), None, None, None, "sc"),
        P(("cell", "ap"), None, None, None, "sc"),
        P("cell"),
        P(("cell", "ap")),
        P(("cell", "ap"), None),
        P("cell"),
        P("cell", None),
        P("cell", None),
    )
    return jax.shard_map(
        functools.partial(local, mesh.shape["ap"], mesh.shape["sc"], ring_functions(mesh)),
        mesh=mesh,
        in_specs=placed,
        out_specs=P(("cell", "ap"), None, None, None, "sc"),
        check_vma=False,
    )
```

time: 44.3 us -> 38.4 us (0.87)
  Pallas kernels: 41.2 us -> 35.9 us
  local copies, waits for them, and re-layouts: 2.88 us -> 2.31 us
    pallas_call x2 -> x1, Pallas kernels: 41.2 us -> 35.9 us  [local(): pl.pallas_call(functools.partial(uplink_kernel, n, chunks, ring_of), out_...]
    unnamed x4 -> x1, local copies, waits for them, and re-layouts: 2.88 us -> 2.31 us
where the time goes in v1:
time: 38.4 us; the launch traced here: 38.2 us
  Pallas kernels  35.9 us (93%)
  local copies, waits for them, and re-layouts  2.31 us (6%)
    pallas_call x1, Pallas kernels, local(): pl.pallas_call(functools.partial(uplink_kernel, n, chunks, ring_of), out_...  35.9 us
    unnamed x1, local copies, waits for them, and re-layouts  2.31 us

profile of v1, /device:TPU:0, one launch (start us, length us, event | category | flops | bytes accessed | tf_op | source)
XLA Modules:
  0.0 38.2 jit_solution(9706174416896377086)
XLA Ops:
  0.0 35.9 %uplink.1 = f32[2048,128]{1,0:T(8,128)} custom-call(bf16[2,4,2,128,1024]{4,3,2,1,0:T(8,128)(2,1)} %guess_hbm.1, bf16[2,4,2,4,1024]{4,3,2,1,0:T(4,128)(2,1)} %received_hbm.1, f32[1,128]{1,0:T(1,128)} %bitcast.10, f32[1,2]{1,0:T(1,128)} %bitcast.11, f32[2,128]{1,0:T(2,128)} %gain_hbm.1, s32[1,128]{1,0:T(1,128)} %bitcast.12, s32[16,16]{1,0:T(8,128)} %serving_hbm.1, ...), custom_call_target="tpu_custom_call" | custom-call | tf_op jit(solution)/shard_map/uplink/pallas_call | solution.py:686
  35.9 2.3 %copy.15 = f32[4,8,4,2,1024]{4,3,2,1,0:T(2,128)} copy(f32[4,8,4,2,1024]{4,3,2,1,0:T(2,128)} %bitcast.9) | data formatting | bytes 2097152

commit v2 on v1

--- a/solution.py
+++ b/solution.py
@@ -81,8 +81,8 @@
 def tap_tables(parts, tones):
     made = []
     for part in range(parts):
-        real, imag = wave_table(part * tones + np.arange(tones, dtype=np.int32))
-        made.append(np.concatenate([real.T, imag.T], axis=0))
+        real, _ = wave_table(part * tones + np.arange(tones, dtype=np.int32))
+        made.append(real.T)
     return np.stack(made).astype(jnp.bfloat16)
 
 
@@ -179,7 +179,9 @@
     table_hbm,
     coarse_hbm,
     spread_hbm,
-    out_ref,
+    share_hbm,
+    place_ref,
+    scale_ref,
     coef_all,
     solved_all,
     received_ref,
@@ -223,6 +225,7 @@
     small_sem,
     relay_send_sem,
     relay_recv_sem,
+    share_sem,
 ):
     stations, antennas, _, users, tones = guess.shape
     pieces = stations * antennas
@@ -250,8 +253,19 @@
     for q in range(pieces):
         a, i = q // antennas, q % antennas
         copy = pltpu.make_async_copy(guess_hbm.at[a, i], guess.at[a, i], guess_sem.at[q])
-        copy.start()
         guess_copies.append(copy)
+    for copy in guess_copies[: pieces // 2]:
+        copy.start()
+    barrier = pltpu.get_barrier_semaphore()
+    pl.semaphore_signal(barrier, inc=1, device_id={"sc": 1 - part}, device_id_type=MESH)
+    for k in range(1, n):
+        pl.semaphore_signal(
+            barrier, inc=1, device_id={"ap": lax.rem(me + k, n)}, device_id_type=MESH
+        )
+
+    table_copies[0].wait()
+    for copy in guess_copies[pieces // 2 :]:
+        copy.start()
     small_copies = []
     for source, into in (
         (cluster_hbm, cluster_ref),
@@ -268,34 +282,37 @@
     for copy in table_copies[1:]:
         copy.start()
 
-    barrier = pltpu.get_barrier_semaphore()
-    pl.semaphore_signal(barrier, inc=1, device_id={"sc": 1 - part}, device_id_type=MESH)
-    for k in range(1, n):
-        pl.semaphore_signal(
-            barrier, inc=1, device_id={"ap": lax.rem(me + k, n)}, device_id_type=MESH
-        )
-
-    table_copies[0].wait()
     half_copies = []
-    for q in range(pieces):
-        a, i = q // antennas, q % antennas
-        guess_copies[q].wait()
-        sums = jnp.dot(
-            guess[a, i, 0], taps[:tones, :], preferred_element_type=jnp.float32
-        ) + jnp.dot(guess[a, i, 1], taps[tones:, :], preferred_element_type=jnp.float32)
-        half[q] = (sums * (1.0 / TONE_NUMBER)).astype(jnp.bfloat16)
-        if q == 0:
+    together = 2
+    lower = lax.broadcasted_iota(jnp.int32, (users, 2 * TAPS), 1) < TAPS
+    for first in range(0, pieces, together):
+        group = range(first, first + together)
+        for q in group:
+            guess_copies[q].wait()
+        a, i = first // antennas, first % antennas
+        products = jnp.dot(
+            guess[a, i : i + together].reshape(together * 2 * users, tones),
+            taps[...],
+            preferred_element_type=jnp.float32,
+        )
+        for q in group:
+            at = (q - first) * 2 * users
+            turned = pltpu.roll(products[at + users : at + 2 * users], TAPS, axis=1)
+            sums = products[at : at + users] + jnp.where(lower, -turned, turned)
+            half[q] = (sums * (1.0 / TONE_NUMBER)).astype(jnp.bfloat16)
+        if first == 0:
             pl.semaphore_wait(barrier, n)
-        copy = pltpu.make_async_remote_copy(
-            src_ref=half.at[q],
-            dst_ref=other.at[q],
-            send_sem=half_send_sem.at[q],
-            recv_sem=half_recv_sem.at[q],
-            device_id={"sc": 1 - part},
-            device_id_type=MESH,
-        )
-        copy.start()
-        half_copies.append(copy)
+        for q in group:
+            copy = pltpu.make_async_remote_copy(
+                src_ref=half.at[q],
+                dst_ref=other.at[q],
+                send_sem=half_send_sem.at[q],
+                recv_sem=half_recv_sem.at[q],
+                device_id={"sc": 1 - part},
+                device_id_type=MESH,
+            )
+            copy.start()
+            half_copies.append(copy)
 
     for copy in small_copies:
         copy.wait()
@@ -485,9 +502,8 @@
             joined = jnp.concatenate([solved[i][0], solved[i][1]], axis=0)
             own[c, pl.ds(i * 2 * rows, 2 * rows), :] = joined.astype(jnp.bfloat16)
         ready.append((me, c, own.at[c]))
-        for d in range(c + 1):
-            for direction in range(2):
-                ring_start(d, direction, c - d)
+        for direction in range(2):
+            ring_start(c, direction, 0)
 
     for copy in gain_copies:
         copy.wait_recv()
@@ -501,7 +517,7 @@
     slot_user = iota((OWN_MAX * CU, users), 0) == jnp.where(held, rank_u * CU + position, -1.0)
     slot_rows = jnp.where(slot_user, 1.0, 0.0)
     slot_scale = jnp.sum(jnp.where(slot_user, scale, 0.0), axis=1, keepdims=True)
-    slot_scale = jnp.broadcast_to(slot_scale, (OWN_MAX * CU, LANES))
+    scale_ref[...] = jnp.broadcast_to(slot_scale, (OWN_MAX * CU, LANES))
     hits = []
     for p in range(n):
         goal = jnp.where(
@@ -509,7 +525,7 @@
         )
         hits.append(jnp.where(iota((block, users), 0) == goal, 1.0, 0.0))
     placement = exact_dot(slot_rows, jnp.concatenate(hits, axis=0), ((1,), (1,)))
-    placement = placement.astype(jnp.bfloat16)
+    place_ref[...] = placement.astype(jnp.bfloat16)
 
     relay_copies = []
     for k in range(1, n):
@@ -571,6 +587,15 @@
                     share[s * 2 + reim, at, pl.ds(c * width + l * LANES, LANES)] = (
                         jnp.concatenate(values, axis=0).astype(jnp.bfloat16)
                     )
+        at = pl.ds(pl.multiple_of(origin * block, block), block)
+        lanes = pl.ds(c * width, width)
+        copy = pltpu.make_async_copy(
+            share.at[:, at, lanes], share_hbm.at[:, at, lanes], share_sem.at[len(share_copies)]
+        )
+        copy.start()
+        share_copies.append(copy)
+
+    share_copies = []
 
     def drain(most):
         for _ in range(most):
@@ -579,32 +604,19 @@
 
     drain(1)
     waited = False
-    for late in range(chunks, chunks + steps):
-        for d in range(chunks):
+    for step in range(1, steps + 1):
+        for c in range(chunks):
             for direction in range(2):
-                if late - d > 0 and ring_start(d, direction, late - d):
-                    if not waited and len(ready) and ready[0][0] is not me:
-                        for copy in relay_copies:
-                            copy.wait_recv()
-                        waited = True
-                    drain(1)
-    if not waited:
-        for copy in relay_copies:
-            copy.wait_recv()
+                if not ring_start(c, direction, step):
+                    continue
+                if not waited and len(ready) and ready[0][0] is not me:
+                    for copy in relay_copies:
+                        copy.wait_recv()
+                    waited = True
+                drain(1)
     drain(len(ready))
-
-    tiles = tones // LANES
-    for s in range(symbols):
-        for reim in range(2):
-            placed = jnp.dot(placement, share[s * 2 + reim], preferred_element_type=jnp.float32)
-            for l in range(tiles):
-                for r in range(OWN_MAX):
-                    value = placed[r * CU : (r + 1) * CU, l * LANES : (l + 1) * LANES]
-                    first = r * CU * symbols * tiles * 2 + (s * tiles + l) * 2 + reim
-                    out_ref[pl.ds(first, CU, stride=symbols * tiles * 2), :] = (
-                        value * slot_scale[r * CU : (r + 1) * CU]
-                    )
-
+    for copy in share_copies:
+        copy.wait()
     for copy in relay_copies:
         copy.wait_send()
     for copy in half_copies:
@@ -615,6 +627,45 @@
         copy.wait_send()
     for copy in ring_copies.values():
         copy.wait_send()
+
+
+def place_kernel(
+    place_hbm, scale_hbm, share_hbm, out_hbm, place_ref, scale_ref, share, lines, small_sem, in_sem, out_sem
+):
+    kinds, _, tones = share.shape
+    smalls = []
+    for source, into in ((place_hbm, place_ref), (scale_hbm, scale_ref)):
+        copy = pltpu.make_async_copy(source, into, small_sem.at[len(smalls)])
+        copy.start()
+        smalls.append(copy)
+    symbols, tiles = kinds // 2, tones // LANES
+    arrivals = []
+    for kind in range(kinds):
+        copy = pltpu.make_async_copy(share_hbm.at[kind], share.at[kind], in_sem.at[kind])
+        copy.start()
+        arrivals.append(copy)
+    for copy in smalls:
+        copy.wait()
+    copies = []
+    for s in range(symbols):
+        for reim in range(2):
+            arrivals[s * 2 + reim].wait()
+            placed = jnp.dot(
+                place_ref[...], share[s * 2 + reim], preferred_element_type=jnp.float32
+            )
+            for l in range(tiles):
+                for r in range(OWN_MAX):
+                    rows = slice(r * CU, (r + 1) * CU)
+                    value = placed[rows, l * LANES : (l + 1) * LANES] * scale_ref[rows]
+                    lines[s, pl.ds(r * CU * 2 * tiles + l * 2 + reim, CU, stride=2 * tiles), :] = value
+        height = 2 * tiles
+        copy = pltpu.make_async_copy(
+            lines.at[s].reshape(OWN_MAX * CU, height, LANES), out_hbm.at[:, s], out_sem.at[s]
+        )
+        copy.start()
+        copies.append(copy)
+    for copy in copies:
+        copy.wait()
 
 
 def ring_functions(mesh):
@@ -682,12 +733,16 @@
     bf16, f32 = jnp.bfloat16, jnp.float32
     hbm = pl.BlockSpec(memory_space=pltpu.HBM)
     tiles = tones // LANES
-    lines = OWN_MAX * CU * symbols * tiles * 2
-    placed = pl.pallas_call(
+    slots = OWN_MAX * CU
+    share, place, scale = pl.pallas_call(
         functools.partial(uplink_kernel, n, chunks, ring_of),
-        out_shape=jax.ShapeDtypeStruct((lines, LANES), f32),
+        out_shape=(
+            jax.ShapeDtypeStruct((symbols * 2, n * block, tones), bf16),
+            jax.ShapeDtypeStruct((slots, n * block), bf16),
+            jax.ShapeDtypeStruct((slots, LANES), f32),
+        ),
         in_specs=[hbm] * 12,
-        out_specs=vmem,
+        out_specs=(hbm, vmem, vmem),
         scratch_shapes=[
             pltpu.VMEM((n, pieces, block, 2 * TAPS), bf16),
             pltpu.VMEM((n, chunks, antennas * 2 * rows, width), bf16),
@@ -700,7 +755,7 @@
             pltpu.VMEM((1, serving.shape[0]), jnp.int32),
             pltpu.VMEM((antennas, 3, rows, width), f32),
             pltpu.VMEM((stations, antennas, 2, users, tones), bf16),
-            pltpu.VMEM((2 * tones, 2 * TAPS), bf16),
+            pltpu.VMEM((tones, 2 * TAPS), bf16),
             pltpu.VMEM((2 * TAPS, 2 * tones), bf16),
             pltpu.VMEM((2 * TAPS, 2 * COARSE), bf16),
             pltpu.VMEM((2 * COARSE, tones), bf16),
@@ -732,6 +787,7 @@
             dma((7,)),
             dma((n,)),
             dma((n,)),
+            dma((n * chunks,)),
         ],
         compiler_params=pltpu.CompilerParams(
             collective_id=0, has_side_effects=True, vmem_limit_bytes=VMEM_BYTES
@@ -751,6 +807,23 @@
         jnp.asarray(coarse_table()),
         jnp.asarray(spread_tables(parts, tones)),
     )
+    placed = pl.pallas_call(
+        place_kernel,
+        out_shape=jax.ShapeDtypeStruct((slots, symbols, tiles * 2, LANES), f32),
+        in_specs=[hbm, hbm, hbm],
+        out_specs=hbm,
+        scratch_shapes=[
+            pltpu.VMEM((slots, n * block), bf16),
+            pltpu.VMEM((slots, LANES), f32),
+            pltpu.VMEM((symbols * 2, n * block, tones), bf16),
+            pltpu.VMEM((symbols, slots * tiles * 2, LANES), f32),
+            dma((2,)),
+            dma((symbols * 2,)),
+            dma((symbols,)),
+        ],
+        compiler_params=pltpu.CompilerParams(vmem_limit_bytes=VMEM_BYTES),
+        name="place",
+    )(place, scale, share)
     placed = placed.reshape(OWN_MAX, CU, symbols, tiles, 2, LANES)
     placed = jnp.transpose(placed, (0, 1, 2, 4, 3, 5))
     return placed.reshape(OWN_MAX, CU, symbols, 2, tones)

time: 38.4 us -> 35 us (0.911)
  local copies, waits for them, and re-layouts: 2.31 us -> 0 us
  Pallas kernels: 35.9 us -> 34.8 us
    pallas_call x1, Pallas kernels: 35.9 us -> 31.3 us  [local(): pl.pallas_call(functools.partial(uplink_kernel, n, chunks, ring_of), out_...]
    pallas_call x0 -> x1, Pallas kernels: none -> 3.55 us  [local(): pl.pallas_call(place_kernel, out_shape=jax.ShapeDtypeStruct((slots, symbo...]
    unnamed x1 -> x0, local copies, waits for them, and re-layouts: 2.31 us -> none
where the time goes in v2:
time: 35 us; the launch traced here: 34.8 us
  Pallas kernels  34.8 us (99%)
    pallas_call x1, Pallas kernels, local(): pl.pallas_call(functools.partial(uplink_kernel, n, chunks, ring_of), out_...  31.3 us
    pallas_call x1, Pallas kernels, local(): pl.pallas_call(place_kernel, out_shape=jax.ShapeDtypeStruct((slots, symbo...  3.55 us

profile of v2, /device:TPU:0, one launch (start us, length us, event | category | flops | bytes accessed | tf_op | source)
XLA Modules:
  0.0 34.8 jit_solution(15489750018403349131)
XLA Ops:
  0.0 31.3 %uplink.1 = (bf16[8,128,1024]{2,1,0:T(8,128)(2,1)}, bf16[32,128]{1,0:T(8,128)(2,1)}, f32[32,128]{1,0:T(8,128)}) custom-call(bf16[2,4,2,128,1024]{4,3,2,1,0:T(8,128)(2,1)} %guess_hbm.1, bf16[2,4,2,4,1024]{4,3,2,1,0:T(4,128)(2,1)} %received_hbm.1, f32[1,128]{1,0:T(1,128)} %bitcast.9, f32[1,2]{1,0:T(1,128)} %bitcast.10, f32[2,128]{1,0:T(2,128)} %gain_hbm.1, ...), custom_call_target="tpu_custom_call" | custom-call | tf_op jit(solution)/shard_map/uplink/pallas_call | solution.py:737
  31.3 3.6 %place.1 = f32[32,4,16,128]{3,2,1,0:T(8,128)} custom-call(bf16[32,128]{1,0:T(8,128)(2,1)} %get-tuple-element.8.place_hbm, f32[32,128]{1,0:T(8,128)} %get-tuple-element.9.scale_hbm, bf16[8,128,1024]{2,1,0:T(8,128)(2,1)} %get-tuple-element.10.share_hbm), custom_call_target="tpu_custom_call" | custom-call | tf_op jit(solution)/shard_map/place/pallas_call | solution.py:810

commit v3 on v2

--- a/solution.py
+++ b/solution.py
@@ -165,7 +165,6 @@
 
 def uplink_kernel(
     n,
-    chunks,
     ring_of,
     guess_hbm,
     received_hbm,
@@ -180,10 +179,10 @@
     coarse_hbm,
     spread_hbm,
     share_hbm,
-    place_ref,
-    scale_ref,
-    coef_all,
-    solved_all,
+    place_hbm,
+    scale_hbm,
+    packet_all,
+    signal_all,
     received_ref,
     power_ref,
     noise_ref,
@@ -191,7 +190,6 @@
     cluster_ref,
     serving_ref,
     owner_ref,
-    solved_wide,
     guess,
     taps,
     table,
@@ -199,7 +197,7 @@
     spread,
     half,
     other,
-    coef_send,
+    packet_send,
     coef_b,
     gains,
     pick,
@@ -208,24 +206,26 @@
     sampled,
     samples,
     cov,
+    solved,
     smooth,
-    own,
     share,
+    place_ref,
+    scale_ref,
     guess_sem,
     table_sem,
     half_send_sem,
     half_recv_sem,
     gain_send_sem,
     gain_recv_sem,
-    coef_send_sem,
-    coef_recv_sem,
+    packet_send_sem,
+    packet_recv_sem,
     ring_send_sem,
     ring_recv_sem,
-    local_sem,
     small_sem,
     relay_send_sem,
     relay_recv_sem,
     share_sem,
+    place_sem,
 ):
     stations, antennas, _, users, tones = guess.shape
     pieces = stations * antennas
@@ -248,6 +248,8 @@
         table_copies.append(
             pltpu.make_async_copy(source, into, table_sem.at[len(table_copies)])
         )
+    received_copy = pltpu.make_async_copy(received_hbm, received_ref, place_sem.at[0])
+    received_copy.start()
     table_copies[0].start()
     guess_copies = []
     for q in range(pieces):
@@ -262,6 +264,39 @@
         pl.semaphore_signal(
             barrier, inc=1, device_id={"ap": lax.rem(me + k, n)}, device_id_type=MESH
         )
+
+    ring_copies = {}
+    reach = {}
+    for c in range(stations):
+        far, near = n // 2, n - 1 - n // 2
+        reach[c] = (far, near) if c % 2 == 0 else (near, far)
+    steps = max(max(r) for r in reach.values())
+
+    def origin_of(direction, step):
+        back = lax.rem(spot + n - step, n) if direction == 0 else lax.rem(spot + step, n)
+        return node(back)
+
+    def ring_step(c, step):
+        for direction in range(2):
+            if step > reach[c][direction]:
+                continue
+            origin = origin_of(direction, step)
+            source = received_ref.at[c]
+            if step > 0:
+                ring_copies[c, direction, step - 1].wait_recv()
+                source = signal_all.at[origin, c]
+            if step == reach[c][direction]:
+                continue
+            copy = pltpu.make_async_remote_copy(
+                src_ref=source,
+                dst_ref=signal_all.at[origin, c],
+                send_sem=ring_send_sem.at[direction, c, step],
+                recv_sem=ring_recv_sem.at[direction, c, step],
+                device_id={"ap": right if direction == 0 else left},
+                device_id_type=MESH,
+            )
+            copy.start()
+            ring_copies[c, direction, step] = copy
 
     table_copies[0].wait()
     for copy in guess_copies[pieces // 2 :]:
@@ -274,7 +309,6 @@
         (power_hbm, power_ref),
         (gain_hbm, gain_ref),
         (noise_hbm, noise_ref),
-        (received_hbm, received_ref),
     ):
         copy = pltpu.make_async_copy(source, into, small_sem.at[len(small_copies)])
         copy.start()
@@ -302,6 +336,9 @@
             half[q] = (sums * (1.0 / TONE_NUMBER)).astype(jnp.bfloat16)
         if first == 0:
             pl.semaphore_wait(barrier, n)
+            received_copy.wait()
+            for c in range(stations):
+                ring_step(c, 0)
         for q in group:
             copy = pltpu.make_async_remote_copy(
                 src_ref=half.at[q],
@@ -351,79 +388,20 @@
     wide = jnp.broadcast_to(power_ref[...] * (1.0 / users), (LANES, users))
     power_wide[...] = jnp.transpose(wide)
 
+    ring_step(0, 1)
     for q in range(pieces):
         half_copies[q].wait_recv()
         total = (half[q].astype(jnp.float32) + other[q].astype(jnp.float32)).astype(jnp.bfloat16)
         coef_b[pl.ds(q * users, users), :] = total
         chosen = jnp.dot(pick[...], total, preferred_element_type=jnp.float32)
         chosen = chosen * pick_weight[q // antennas]
-        coef_send[:, q] = chosen.astype(jnp.bfloat16).reshape(n, block, 2 * TAPS)
-    coef_copies = []
-    mine_half = pl.ds(part * (pieces // 2), pieces // 2)
-    for k in range(1, n):
-        peer = lax.rem(me + k, n)
-        copy = pltpu.make_async_remote_copy(
-            src_ref=coef_send.at[peer, mine_half],
-            dst_ref=coef_all.at[me, mine_half],
-            send_sem=coef_send_sem.at[k],
-            recv_sem=coef_recv_sem.at[n - k],
-            device_id={"ap": peer},
-            device_id_type=MESH,
-        )
-        copy.start()
-        coef_copies.append(copy)
-    own_coef = pltpu.make_async_copy(coef_send.at[me], coef_all.at[me], local_sem)
-    own_coef.start()
-
-    width = tones // chunks
-    lane_tiles = width // LANES
+        packet_send[:, q] = chosen.astype(jnp.bfloat16).reshape(n, block, 2 * TAPS)
     symbols = received_ref.shape[3]
     rows = stations * symbols
-    ring_copies = {}
-    reach = {}
-    for c in range(chunks):
-        far, near = n // 2, n - 1 - n // 2
-        reach[c] = (far, near) if c % 2 == 0 else (near, far)
-
-    ready = []
-
-    def origin_of(direction, step):
-        back = lax.rem(spot + n - step, n) if direction == 0 else lax.rem(spot + step, n)
-        return node(back)
-
-    def ring_start(c, direction, step):
-        if step > reach[c][direction]:
-            return False
-        origin = origin_of(direction, step)
-        source = own.at[c]
-        if step > 0:
-            ring_copies[c, direction, step - 1].wait_recv()
-            source = solved_all.at[origin, c]
-            ready.append((origin, c, source))
-        if step == reach[c][direction]:
-            return True
-        copy = pltpu.make_async_remote_copy(
-            src_ref=source,
-            dst_ref=solved_all.at[origin, c],
-            send_sem=ring_send_sem.at[direction, c, step],
-            recv_sem=ring_recv_sem.at[direction, c, step],
-            device_id={"ap": right if direction == 0 else left},
-            device_id_type=MESH,
-        )
-        copy.start()
-        ring_copies[c, direction, step] = copy
-        return True
-
-    steps = max(max(r) for r in reach.values())
     entries = [(i, j) for i in range(antennas) for j in range(i + 1)]
-    noise = jnp.concatenate(
-        [
-            jnp.broadcast_to(noise_ref[0:1, a : a + 1], (symbols, 1))
-            for a in range(stations)
-        ],
-        axis=0,
-    )
-
+    kinds = antennas * antennas
+    for c in range(1, stations):
+        ring_step(c, 1)
     for copy in table_copies[1:]:
         copy.wait()
     both = jnp.dot(coef_b[...], coarse[...], preferred_element_type=jnp.float32)
@@ -454,57 +432,171 @@
 
         zero = jnp.zeros((8, COARSE), jnp.float32)
         sums = lax.fori_loop(0, users // 16, body, (zero,) * (antennas * antennas))
-        for e in range(antennas * antennas):
-            value = jnp.sum(sums[e], axis=0, keepdims=True)
-            samples[pl.ds(e * rows + a * symbols, symbols), :] = jnp.broadcast_to(
-                value, (symbols, COARSE)
-            )
+        at = 0
+        for i, j in entries:
+            for reim in range(1 if i == j else 2):
+                value = jnp.sum(sums[at], axis=0, keepdims=True)
+                if i == j:
+                    value = value + noise_ref[0:1, a : a + 1]
+                samples[pl.ds(at * stations + a, 1), :] = value
+                at += 1
     high = samples[...].astype(jnp.bfloat16)
     low = (samples[...] - high.astype(jnp.float32)).astype(jnp.bfloat16)
-    cov[...] = (
-        jnp.dot(
+    held_rows = kinds * stations // block
+    for k in range(n):
+        packet_send[k, pieces : pieces + held_rows] = high.reshape(held_rows, block, COARSE)
+        packet_send[k, pieces + held_rows :] = low.reshape(held_rows, block, COARSE)
+    parcels = packet_send.shape[1]
+    mine_half = pl.ds(part * (parcels // 2), parcels // 2)
+    packets = {}
+    for step in range(1, steps + 1):
+        for k in sorted({step, n - step}):
+            peer = node(lax.rem(spot + k, n))
+            copy = pltpu.make_async_remote_copy(
+                src_ref=packet_send.at[peer, mine_half],
+                dst_ref=packet_all.at[me, mine_half],
+                send_sem=packet_send_sem.at[k],
+                recv_sem=packet_recv_sem.at[k],
+                device_id={"ap": peer},
+                device_id_type=MESH,
+            )
+            copy.start()
+            packets[k] = copy
+
+    relays = {}
+
+    def relay_start(step):
+        for k in sorted({step, n - step}):
+            packets[k].wait_recv()
+            origin = node(lax.rem(spot + n - k, n))
+            copy = pltpu.make_async_remote_copy(
+                src_ref=packet_all.at[origin, mine_half],
+                dst_ref=packet_all.at[origin, mine_half],
+                send_sem=relay_send_sem.at[k],
+                recv_sem=relay_recv_sem.at[k],
+                device_id={"sc": 1 - part},
+                device_id_type=MESH,
+            )
+            copy.start()
+            relays[k] = copy
+
+    def relay_wait(step):
+        for k in sorted({step, n - step}):
+            relays[k].wait_recv()
+
+    tiles = tones // LANES
+    station_of = lax.broadcasted_iota(jnp.int32, (rows, 1), 0)
+
+    def prepare(origin, packet, signals, slot):
+        high = packet[pieces : pieces + held_rows].reshape(kinds * stations, COARSE)
+        low = packet[pieces + held_rows :].reshape(kinds * stations, COARSE)
+        cov[slot] = jnp.dot(
             jnp.concatenate([high, high], axis=1),
             spread[...],
             preferred_element_type=jnp.float32,
+        ) + jnp.dot(low, spread[:COARSE, :], preferred_element_type=jnp.float32)
+        width = min(tones, 4 * LANES)
+        for base in range(0, tones, width):
+            lanes = slice(base, base + width)
+
+            def entry(at):
+                value = jnp.broadcast_to(
+                    cov[slot, at * stations : at * stations + 1, lanes], (rows, width)
+                )
+                for a in range(1, stations):
+                    row = jnp.broadcast_to(
+                        cov[slot, at * stations + a : at * stations + a + 1, lanes], (rows, width)
+                    )
+                    value = jnp.where(station_of < a * symbols, value, row)
+                return value
+
+            cov_re = [[None] * antennas for _ in range(antennas)]
+            cov_im = [[None] * antennas for _ in range(antennas)]
+            at = 0
+            for i, j in entries:
+                cov_re[i][j] = entry(at)
+                at += 1
+                if i != j:
+                    cov_im[i][j] = entry(at)
+                    at += 1
+            right_side = []
+            for i in range(antennas):
+                right_side.append(
+                    tuple(
+                        jnp.concatenate(
+                            [
+                                signals[a, i, reim, :, lanes].astype(jnp.float32)
+                                for a in range(stations)
+                            ],
+                            axis=0,
+                        )
+                        for reim in range(2)
+                    )
+                )
+            answer = hermitian_solve(cov_re, cov_im, right_side)
+            for i in range(antennas):
+                re, im = answer[i]
+                solved[slot, i, 0, :, lanes] = re
+                solved[slot, i, 1, :, lanes] = im
+                solved[slot, i, 2, :, lanes] = re + im
+
+    def combine(origin, packet, slot):
+        coefs = packet[:pieces].reshape(pieces * block, 2 * TAPS)
+        for l in range(tiles):
+            columns = pl.ds(l * 2 * LANES, 2 * LANES)
+            smooth[slot, l] = jnp.dot(coefs, table[:, columns], preferred_element_type=jnp.float32)
+        here = pl.ds(pl.multiple_of(origin * block, block), block)
+        for l in range(tiles):
+            lanes = pl.ds(l * LANES, LANES)
+            sums = [[None] * symbols for _ in range(PEER_MAX)]
+            for a in range(stations):
+                for i in range(antennas):
+                    re, im, gap = [], [], []
+                    for k in range(PEER_MAX):
+                        at = (a * antennas + i) * block + k * CU
+                        re.append(smooth[slot, l, pl.ds(at, CU), :LANES])
+                        im.append(smooth[slot, l, pl.ds(at, CU), LANES:])
+                        gap.append(re[k] - im[k])
+                    for s in range(symbols):
+                        row = pl.ds(a * symbols + s, 1)
+                        sre = solved[slot, i, 0, row, lanes]
+                        sim = solved[slot, i, 1, row, lanes]
+                        ssum = solved[slot, i, 2, row, lanes]
+                        for k in range(PEER_MAX):
+                            new = (re[k] * sre, im[k] * sim, gap[k] * ssum)
+                            old = sums[k][s]
+                            if old is not None:
+                                new = tuple(x + y for x, y in zip(old, new))
+                            sums[k][s] = new
+            for s in range(symbols):
+                first = [sums[k][s][0] + sums[k][s][1] for k in range(PEER_MAX)]
+                second = [
+                    sums[k][s][2] - (sums[k][s][0] - sums[k][s][1]) for k in range(PEER_MAX)
+                ]
+                for reim, values in ((0, first), (1, second)):
+                    share[s * 2 + reim, here, lanes] = jnp.concatenate(values, axis=0).astype(
+                        jnp.bfloat16
+                    )
+
+    share_copies = []
+
+    def send_share(origin):
+        here = pl.ds(pl.multiple_of(origin * block, block), block)
+        copy = pltpu.make_async_copy(
+            share.at[:, here], share_hbm.at[:, here], share_sem.at[len(share_copies)]
         )
-        + jnp.dot(low, spread[:COARSE, :], preferred_element_type=jnp.float32)
-    )
-    for c in range(chunks):
-        base = c * width
-        lanes = slice(base, base + width)
-        cov_re = [[None] * antennas for _ in range(antennas)]
-        cov_im = [[None] * antennas for _ in range(antennas)]
-        at = 0
-        for i, j in entries:
-            cov_re[i][j] = cov[at * rows : (at + 1) * rows, lanes]
-            at += 1
-            if i == j:
-                cov_re[i][j] = cov_re[i][j] + noise
-            else:
-                cov_im[i][j] = cov[at * rows : (at + 1) * rows, lanes]
-                at += 1
-        signal = []
-        for i in range(antennas):
-            signal.append(
-                tuple(
-                    jnp.concatenate(
-                        [
-                            received_ref[a, i, reim, :, lanes].astype(jnp.float32)
-                            for a in range(stations)
-                        ],
-                        axis=0,
-                    )
-                    for reim in range(2)
-                )
-            )
-        solved = hermitian_solve(cov_re, cov_im, signal)
-        for i in range(antennas):
-            joined = jnp.concatenate([solved[i][0], solved[i][1]], axis=0)
-            own[c, pl.ds(i * 2 * rows, 2 * rows), :] = joined.astype(jnp.bfloat16)
-        ready.append((me, c, own.at[c]))
-        for direction in range(2):
-            ring_start(c, direction, 0)
-
+        copy.start()
+        share_copies.append(copy)
+
+    tasks = [(me, packet_send.at[me], received_ref, 0)]
+    for step in range(1, steps + 1):
+        for direction in range(2 if step <= n - 1 - n // 2 else 1):
+            origin = origin_of(direction, step)
+            tasks.append((origin, packet_all.at[origin], signal_all.at[origin], step))
+
+    prepare(*tasks[0][:3], 0)
+    combine(*tasks[0][:2], 0)
+    send_share(me)
     for copy in gain_copies:
         copy.wait_recv()
     totals = jnp.zeros((1, users), jnp.float32)
@@ -526,104 +618,43 @@
         hits.append(jnp.where(iota((block, users), 0) == goal, 1.0, 0.0))
     placement = exact_dot(slot_rows, jnp.concatenate(hits, axis=0), ((1,), (1,)))
     place_ref[...] = placement.astype(jnp.bfloat16)
-
-    relay_copies = []
-    for k in range(1, n):
-        coef_copies[n - k - 1].wait_recv()
-        origin = lax.rem(me + n - (n - k), n)
-        copy = pltpu.make_async_remote_copy(
-            src_ref=coef_all.at[origin, mine_half],
-            dst_ref=coef_all.at[origin, mine_half],
-            send_sem=relay_send_sem.at[k],
-            recv_sem=relay_recv_sem.at[k],
-            device_id={"sc": 1 - part},
-            device_id_type=MESH,
-        )
-        copy.start()
-        relay_copies.append(copy)
-    own_coef.wait()
-
-    def combine(origin, c, source):
-        wide = source[...].astype(jnp.float32)
-        for i in range(antennas):
-            re = wide[i * 2 * rows : i * 2 * rows + rows]
-            im = wide[i * 2 * rows + rows : (i + 1) * 2 * rows]
-            solved_wide[i, 0] = re
-            solved_wide[i, 1] = im
-            solved_wide[i, 2] = re + im
-        coefs = coef_all[origin].reshape(pieces * block, 2 * TAPS)
-        for l in range(lane_tiles):
-            columns = pl.ds((c * lane_tiles + l) * 2 * LANES, 2 * LANES)
-            smooth[l] = jnp.dot(coefs, table[:, columns], preferred_element_type=jnp.float32)
-        for l in range(lane_tiles):
-            lanes = pl.ds(l * LANES, LANES)
-            sums = [[None] * symbols for _ in range(PEER_MAX)]
-            for a in range(stations):
-                for i in range(antennas):
-                    re, im, gap = [], [], []
-                    for k in range(PEER_MAX):
-                        at = (a * antennas + i) * block + k * CU
-                        re.append(smooth[l, pl.ds(at, CU), :LANES])
-                        im.append(smooth[l, pl.ds(at, CU), LANES:])
-                        gap.append(re[k] - im[k])
-                    for s in range(symbols):
-                        row = pl.ds(a * symbols + s, 1)
-                        sre = solved_wide[i, 0, row, lanes]
-                        sim = solved_wide[i, 1, row, lanes]
-                        ssum = solved_wide[i, 2, row, lanes]
-                        for k in range(PEER_MAX):
-                            new = (re[k] * sre, im[k] * sim, gap[k] * ssum)
-                            old = sums[k][s]
-                            if old is not None:
-                                new = tuple(x + y for x, y in zip(old, new))
-                            sums[k][s] = new
-            at = pl.ds(pl.multiple_of(origin * block, block), block)
-            for s in range(symbols):
-                first = [sums[k][s][0] + sums[k][s][1] for k in range(PEER_MAX)]
-                second = [
-                    sums[k][s][2] - (sums[k][s][0] - sums[k][s][1]) for k in range(PEER_MAX)
-                ]
-                for reim, values in ((0, first), (1, second)):
-                    share[s * 2 + reim, at, pl.ds(c * width + l * LANES, LANES)] = (
-                        jnp.concatenate(values, axis=0).astype(jnp.bfloat16)
-                    )
-        at = pl.ds(pl.multiple_of(origin * block, block), block)
-        lanes = pl.ds(c * width, width)
-        copy = pltpu.make_async_copy(
-            share.at[:, at, lanes], share_hbm.at[:, at, lanes], share_sem.at[len(share_copies)]
-        )
-        copy.start()
-        share_copies.append(copy)
-
-    share_copies = []
-
-    def drain(most):
-        for _ in range(most):
-            if ready:
-                combine(*ready.pop(0))
-
-    drain(1)
-    waited = False
-    for step in range(1, steps + 1):
-        for c in range(chunks):
-            for direction in range(2):
-                if not ring_start(c, direction, step):
-                    continue
-                if not waited and len(ready) and ready[0][0] is not me:
-                    for copy in relay_copies:
-                        copy.wait_recv()
-                    waited = True
-                drain(1)
-    drain(len(ready))
-    for copy in share_copies:
+    place_copies = []
+    for source, into in ((place_ref, place_hbm), (scale_ref, scale_hbm)):
+        copy = pltpu.make_async_copy(source, into, place_sem.at[1 + len(place_copies)])
+        copy.start()
+        place_copies.append(copy)
+
+    def advance(step, c):
+        if step <= steps:
+            ring_step(c, step)
+
+    relay_start(1)
+    for c in range(stations):
+        advance(2, c)
+    relay_wait(1)
+    prepare(*tasks[1][:3], 1)
+    for t in range(1, len(tasks)):
+        origin, packet, _, step = tasks[t]
+        last = t + 1 == len(tasks)
+        if not last and tasks[t + 1][3] > step:
+            relay_start(step + 1)
+            for c in range(stations):
+                if step + 1 > 2:
+                    advance(step + 1, c)
+            relay_wait(step + 1)
+        combine(origin, packet, t % 2)
+        if not last:
+            prepare(*tasks[t + 1][:3], (t + 1) % 2)
+        send_share(origin)
+    for copy in share_copies + place_copies:
         copy.wait()
-    for copy in relay_copies:
+    for copy in relays.values():
         copy.wait_send()
     for copy in half_copies:
         copy.wait_send()
     for copy in gain_copies:
         copy.wait_send()
-    for copy in coef_copies:
+    for copy in packets.values():
         copy.wait_send()
     for copy in ring_copies.values():
         copy.wait_send()
@@ -725,27 +756,25 @@
     pieces = stations * antennas
     block = PEER_MAX * CU
     rows = stations * symbols
-    chunks = 2
-    width = tones // chunks
+    parcels = pieces + 2 * (antennas * antennas * stations // block)
     steps = n // 2
-    vmem = pl.BlockSpec(memory_space=pltpu.VMEM)
     dma = pltpu.SemaphoreType.DMA
     bf16, f32 = jnp.bfloat16, jnp.float32
     hbm = pl.BlockSpec(memory_space=pltpu.HBM)
     tiles = tones // LANES
     slots = OWN_MAX * CU
     share, place, scale = pl.pallas_call(
-        functools.partial(uplink_kernel, n, chunks, ring_of),
+        functools.partial(uplink_kernel, n, ring_of),
         out_shape=(
             jax.ShapeDtypeStruct((symbols * 2, n * block, tones), bf16),
             jax.ShapeDtypeStruct((slots, n * block), bf16),
             jax.ShapeDtypeStruct((slots, LANES), f32),
         ),
         in_specs=[hbm] * 12,
-        out_specs=(hbm, vmem, vmem),
+        out_specs=(hbm, hbm, hbm),
         scratch_shapes=[
-            pltpu.VMEM((n, pieces, block, 2 * TAPS), bf16),
-            pltpu.VMEM((n, chunks, antennas * 2 * rows, width), bf16),
+            pltpu.VMEM((n, parcels, block, 2 * TAPS), bf16),
+            pltpu.VMEM((n,) + received.shape, bf16),
             pltpu.VMEM(received.shape, bf16),
             pltpu.VMEM((1, users), f32),
             pltpu.VMEM((1, stations), f32),
@@ -753,7 +782,6 @@
             pltpu.VMEM((1, users), jnp.int32),
             pltpu.VMEM(serving.shape, jnp.int32),
             pltpu.VMEM((1, serving.shape[0]), jnp.int32),
-            pltpu.VMEM((antennas, 3, rows, width), f32),
             pltpu.VMEM((stations, antennas, 2, users, tones), bf16),
             pltpu.VMEM((tones, 2 * TAPS), bf16),
             pltpu.VMEM((2 * TAPS, 2 * tones), bf16),
@@ -761,18 +789,20 @@
             pltpu.VMEM((2 * COARSE, tones), bf16),
             pltpu.VMEM((pieces, users, 2 * TAPS), bf16),
             pltpu.VMEM((pieces, users, 2 * TAPS), bf16),
-            pltpu.VMEM((n, pieces, block, 2 * TAPS), bf16),
+            pltpu.VMEM((n, parcels, block, 2 * TAPS), bf16),
             pltpu.VMEM((pieces * users, 2 * TAPS), bf16),
             pltpu.VMEM((n, stations, users), f32),
             pltpu.VMEM((n * block, users), bf16),
             pltpu.VMEM((stations, n * block, LANES), f32),
             pltpu.VMEM((users, LANES), f32),
             pltpu.VMEM((2, pieces * users, COARSE), f32),
-            pltpu.VMEM((antennas * antennas * rows, COARSE), f32),
-            pltpu.VMEM((antennas * antennas * rows, tones), f32),
-            pltpu.VMEM((width // LANES, pieces * block, 2 * LANES), f32),
-            pltpu.VMEM((chunks, antennas * 2 * rows, width), bf16),
+            pltpu.VMEM((antennas * antennas * stations, COARSE), f32),
+            pltpu.VMEM((2, antennas * antennas * stations, tones), f32),
+            pltpu.VMEM((2, antennas, 3, rows, tones), f32),
+            pltpu.VMEM((2, tiles, pieces * block, 2 * LANES), f32),
             pltpu.VMEM((symbols * 2, n * block, tones), bf16),
+            pltpu.VMEM((slots, n * block), bf16),
+            pltpu.VMEM((slots, LANES), f32),
             dma((pieces,)),
             dma((4,)),
             dma((pieces,)),
@@ -781,13 +811,13 @@
             dma((n,)),
             dma((n,)),
             dma((n,)),
-            dma((2, chunks, steps)),
-            dma((2, chunks, steps)),
-            dma,
-            dma((7,)),
+            dma((2, stations, steps)),
+            dma((2, stations, steps)),
+            dma((6,)),
             dma((n,)),
             dma((n,)),
-            dma((n * chunks,)),
+            dma((n,)),
+            dma((3,)),
         ],
         compiler_params=pltpu.CompilerParams(
             collective_id=0, has_side_effects=True, vmem_limit_bytes=VMEM_BYTES

time: 35 us -> 31.3 us (0.89)
  Pallas kernels: 34.8 us -> 31.2 us
    pallas_call x1, Pallas kernels: 31.3 us -> 27.6 us  [local(): pl.pallas_call(functools.partial(uplink_kernel, n, ring_of), out_shape=(j...]
where the time goes in v3:
time: 31.3 us; the launch traced here: 31.2 us
  Pallas kernels  31.2 us (100%)
    pallas_call x1, Pallas kernels, local(): pl.pallas_call(functools.partial(uplink_kernel, n, ring_of), out_shape=(j...  27.6 us
    pallas_call x1, Pallas kernels, local(): pl.pallas_call(place_kernel, out_shape=jax.ShapeDtypeStruct((slots, symbo...  3.55 us

profile of v3, /device:TPU:0, one launch (start us, length us, event | category | flops | bytes accessed | tf_op | source)
XLA Modules:
  0.0 31.2 jit_solution(5691447806867892126)
XLA Ops:
  0.0 27.6 %uplink.1 = (bf16[8,128,1024]{2,1,0:T(8,128)(2,1)}, bf16[32,128]{1,0:T(8,128)(2,1)}, f32[32,128]{1,0:T(8,128)}) custom-call(bf16[2,4,2,128,1024]{4,3,2,1,0:T(8,128)(2,1)} %guess_hbm.1, bf16[2,4,2,4,1024]{4,3,2,1,0:T(4,128)(2,1)} %received_hbm.1, f32[1,128]{1,0:T(1,128)} %bitcast.9, f32[1,2]{1,0:T(1,128)} %bitcast.10, f32[2,128]{1,0:T(2,128)} %gain_hbm.1, ...), custom_call_target="tpu_custom_call" | custom-call | tf_op jit(solution)/shard_map/uplink/pallas_call | solution.py:766
  27.6 3.6 %place.1 = f32[32,4,16,128]{3,2,1,0:T(8,128)} custom-call(bf16[32,128]{1,0:T(8,128)(2,1)} %get-tuple-element.8.place_hbm, f32[32,128]{1,0:T(8,128)} %get-tuple-element.9.scale_hbm, bf16[8,128,1024]{2,1,0:T(8,128)(2,1)} %get-tuple-element.10.share_hbm), custom_call_target="tpu_custom_call" | custom-call | tf_op jit(solution)/shard_map/place/pallas_call | solution.py:840

commit v4 on v3

--- a/solution.py
+++ b/solution.py
@@ -182,6 +182,7 @@
     place_hbm,
     scale_hbm,
     packet_all,
+    sample_all,
     signal_all,
     received_ref,
     power_ref,
@@ -198,6 +199,7 @@
     half,
     other,
     packet_send,
+    sample_send,
     coef_b,
     gains,
     pick,
@@ -219,6 +221,8 @@
     gain_recv_sem,
     packet_send_sem,
     packet_recv_sem,
+    sample_send_sem,
+    sample_recv_sem,
     ring_send_sem,
     ring_recv_sem,
     small_sem,
@@ -248,22 +252,60 @@
         table_copies.append(
             pltpu.make_async_copy(source, into, table_sem.at[len(table_copies)])
         )
-    received_copy = pltpu.make_async_copy(received_hbm, received_ref, place_sem.at[0])
-    received_copy.start()
+    small_copies = []
+    for source, into in (
+        (cluster_hbm, cluster_ref),
+        (serving_hbm, serving_ref),
+        (owner_hbm, owner_ref),
+        (power_hbm, power_ref),
+        (gain_hbm, gain_ref),
+        (noise_hbm, noise_ref),
+    ):
+        copy = pltpu.make_async_copy(source, into, small_sem.at[len(small_copies)])
+        copy.start()
+        small_copies.append(copy)
     table_copies[0].start()
     guess_copies = []
     for q in range(pieces):
         a, i = q // antennas, q % antennas
         copy = pltpu.make_async_copy(guess_hbm.at[a, i], guess.at[a, i], guess_sem.at[q])
         guess_copies.append(copy)
-    for copy in guess_copies[: pieces // 2]:
+    for copy in guess_copies:
         copy.start()
+    received_copy = pltpu.make_async_copy(received_hbm, received_ref, place_sem.at[0])
+    received_copy.start()
+    for copy in table_copies[1:]:
+        copy.start()
+
     barrier = pltpu.get_barrier_semaphore()
     pl.semaphore_signal(barrier, inc=1, device_id={"sc": 1 - part}, device_id_type=MESH)
     for k in range(1, n):
         pl.semaphore_signal(
             barrier, inc=1, device_id={"ap": lax.rem(me + k, n)}, device_id_type=MESH
         )
+
+    for copy in small_copies:
+        copy.wait()
+    owner_u, rank_u, served_u, before_u, serve_u, position = user_tables(
+        cluster_ref[...], serving_ref[...], owner_ref[...], clusters, users, stations, n
+    )
+    mef = me.astype(jnp.float32)
+    mine = iota((n, users), 0) == mef
+    served_me = jnp.sum(jnp.where(mine, served_u, 0.0), axis=0, keepdims=True)
+    before_me = jnp.sum(jnp.where(mine, before_u, 0.0), axis=0, keepdims=True)
+    target = jnp.where(
+        served_me > 0.5, owner_u * block + before_me * CU + position, -1.0
+    )
+    chosen_user = iota((n * block, users), 0) == target
+    pick[...] = jnp.where(chosen_user, 1.0, 0.0).astype(jnp.bfloat16)
+    for a in range(stations):
+        row_here = iota((n * stations, users), 0) == mef * stations + a
+        weight = jnp.sum(jnp.where(row_here, serve_u, 0.0), axis=0, keepdims=True)
+        weight = weight * gain_ref[a : a + 1, :]
+        column = jnp.sum(jnp.where(chosen_user, weight, 0.0), axis=1, keepdims=True)
+        pick_weight[a] = jnp.broadcast_to(column, (n * block, LANES))
+    wide = jnp.broadcast_to(power_ref[...] * (1.0 / users), (LANES, users))
+    power_wide[...] = jnp.transpose(wide)
 
     ring_copies = {}
     reach = {}
@@ -299,60 +341,35 @@
             ring_copies[c, direction, step] = copy
 
     table_copies[0].wait()
-    for copy in guess_copies[pieces // 2 :]:
+    for copy in guess_copies:
+        copy.wait()
+    count = pieces * users
+    lower = lax.broadcasted_iota(jnp.int32, (count, 2 * TAPS), 1) < TAPS
+    products = [
+        jnp.dot(
+            guess[:, :, reim].reshape(count, tones), taps[...], preferred_element_type=jnp.float32
+        )
+        for reim in range(2)
+    ]
+    turned = pltpu.roll(products[1], TAPS, axis=1)
+    sums = products[0] + jnp.where(lower, -turned, turned)
+    half[...] = (sums * (1.0 / TONE_NUMBER)).astype(jnp.bfloat16).reshape(half.shape)
+    received_copy.wait()
+    pl.semaphore_wait(barrier, n)
+    for c in range(stations):
+        ring_step(c, 0)
+    half_copies = []
+    for q in range(pieces):
+        copy = pltpu.make_async_remote_copy(
+            src_ref=half.at[q],
+            dst_ref=other.at[q],
+            send_sem=half_send_sem.at[q],
+            recv_sem=half_recv_sem.at[q],
+            device_id={"sc": 1 - part},
+            device_id_type=MESH,
+        )
         copy.start()
-    small_copies = []
-    for source, into in (
-        (cluster_hbm, cluster_ref),
-        (serving_hbm, serving_ref),
-        (owner_hbm, owner_ref),
-        (power_hbm, power_ref),
-        (gain_hbm, gain_ref),
-        (noise_hbm, noise_ref),
-    ):
-        copy = pltpu.make_async_copy(source, into, small_sem.at[len(small_copies)])
-        copy.start()
-        small_copies.append(copy)
-    for copy in table_copies[1:]:
-        copy.start()
-
-    half_copies = []
-    together = 2
-    lower = lax.broadcasted_iota(jnp.int32, (users, 2 * TAPS), 1) < TAPS
-    for first in range(0, pieces, together):
-        group = range(first, first + together)
-        for q in group:
-            guess_copies[q].wait()
-        a, i = first // antennas, first % antennas
-        products = jnp.dot(
-            guess[a, i : i + together].reshape(together * 2 * users, tones),
-            taps[...],
-            preferred_element_type=jnp.float32,
-        )
-        for q in group:
-            at = (q - first) * 2 * users
-            turned = pltpu.roll(products[at + users : at + 2 * users], TAPS, axis=1)
-            sums = products[at : at + users] + jnp.where(lower, -turned, turned)
-            half[q] = (sums * (1.0 / TONE_NUMBER)).astype(jnp.bfloat16)
-        if first == 0:
-            pl.semaphore_wait(barrier, n)
-            received_copy.wait()
-            for c in range(stations):
-                ring_step(c, 0)
-        for q in group:
-            copy = pltpu.make_async_remote_copy(
-                src_ref=half.at[q],
-                dst_ref=other.at[q],
-                send_sem=half_send_sem.at[q],
-                recv_sem=half_recv_sem.at[q],
-                device_id={"sc": 1 - part},
-                device_id_type=MESH,
-            )
-            copy.start()
-            half_copies.append(copy)
-
-    for copy in small_copies:
-        copy.wait()
+        half_copies.append(copy)
     gain_copies = []
     for k in range(1, n):
         peer = lax.rem(me + k, n)
@@ -367,46 +384,49 @@
         copy.start()
         gain_copies.append(copy)
     gains[me] = gain_ref[...]
-    owner_u, rank_u, served_u, before_u, serve_u, position = user_tables(
-        cluster_ref[...], serving_ref[...], owner_ref[...], clusters, users, stations, n
-    )
-    mef = me.astype(jnp.float32)
-    mine = iota((n, users), 0) == mef
-    served_me = jnp.sum(jnp.where(mine, served_u, 0.0), axis=0, keepdims=True)
-    before_me = jnp.sum(jnp.where(mine, before_u, 0.0), axis=0, keepdims=True)
-    target = jnp.where(
-        served_me > 0.5, owner_u * block + before_me * CU + position, -1.0
-    )
-    chosen_user = iota((n * block, users), 0) == target
-    pick[...] = jnp.where(chosen_user, 1.0, 0.0).astype(jnp.bfloat16)
-    for a in range(stations):
-        row_here = iota((n * stations, users), 0) == mef * stations + a
-        weight = jnp.sum(jnp.where(row_here, serve_u, 0.0), axis=0, keepdims=True)
-        weight = weight * gain_ref[a : a + 1, :]
-        column = jnp.sum(jnp.where(chosen_user, weight, 0.0), axis=1, keepdims=True)
-        pick_weight[a] = jnp.broadcast_to(column, (n * block, LANES))
-    wide = jnp.broadcast_to(power_ref[...] * (1.0 / users), (LANES, users))
-    power_wide[...] = jnp.transpose(wide)
-
-    ring_step(0, 1)
+    sums = []
     for q in range(pieces):
         half_copies[q].wait_recv()
         total = (half[q].astype(jnp.float32) + other[q].astype(jnp.float32)).astype(jnp.bfloat16)
         coef_b[pl.ds(q * users, users), :] = total
-        chosen = jnp.dot(pick[...], total, preferred_element_type=jnp.float32)
-        chosen = chosen * pick_weight[q // antennas]
-        packet_send[:, q] = chosen.astype(jnp.bfloat16).reshape(n, block, 2 * TAPS)
+        sums.append(total)
     symbols = received_ref.shape[3]
     rows = stations * symbols
     entries = [(i, j) for i in range(antennas) for j in range(i + 1)]
     kinds = antennas * antennas
-    for c in range(1, stations):
-        ring_step(c, 1)
     for copy in table_copies[1:]:
         copy.wait()
     both = jnp.dot(coef_b[...], coarse[...], preferred_element_type=jnp.float32)
     for reim in range(2):
         sampled[reim] = both[:, reim * COARSE : (reim + 1) * COARSE]
+    chosen = jnp.dot(
+        pick[...], jnp.concatenate(sums, axis=1), preferred_element_type=jnp.float32
+    )
+    for q in range(pieces):
+        values = chosen[:, q * 2 * TAPS : (q + 1) * 2 * TAPS] * pick_weight[q // antennas]
+        packet_send[:, q] = values.astype(jnp.bfloat16).reshape(n, block, 2 * TAPS)
+    mine_half = pl.ds(part * (pieces // 2), pieces // 2)
+
+    def spread_out(send, recv, window, send_sem, recv_sem, each):
+        copies = {}
+        for step in range(1, steps + 1):
+            for k in sorted({step, n - step}):
+                peer = node(lax.rem(spot + k, n))
+                copy = pltpu.make_async_remote_copy(
+                    src_ref=send.at[peer, window] if each else send,
+                    dst_ref=recv.at[me, window] if each else recv.at[me],
+                    send_sem=send_sem.at[k],
+                    recv_sem=recv_sem.at[k],
+                    device_id={"ap": peer},
+                    device_id_type=MESH,
+                )
+                copy.start()
+                copies[k] = copy
+        return copies
+
+    packets = spread_out(
+        packet_send, packet_all, mine_half, packet_send_sem, packet_recv_sem, True
+    )
     for a in range(stations):
 
         def body(step, sums, a=a):
@@ -442,26 +462,15 @@
                 at += 1
     high = samples[...].astype(jnp.bfloat16)
     low = (samples[...] - high.astype(jnp.float32)).astype(jnp.bfloat16)
-    held_rows = kinds * stations // block
-    for k in range(n):
-        packet_send[k, pieces : pieces + held_rows] = high.reshape(held_rows, block, COARSE)
-        packet_send[k, pieces + held_rows :] = low.reshape(held_rows, block, COARSE)
-    parcels = packet_send.shape[1]
-    mine_half = pl.ds(part * (parcels // 2), parcels // 2)
-    packets = {}
-    for step in range(1, steps + 1):
+    sample_send[: kinds * stations] = high
+    sample_send[kinds * stations :] = low
+    sample_copies = spread_out(
+        sample_send, sample_all, None, sample_send_sem, sample_recv_sem, False
+    )
+
+    def sample_wait(step):
         for k in sorted({step, n - step}):
-            peer = node(lax.rem(spot + k, n))
-            copy = pltpu.make_async_remote_copy(
-                src_ref=packet_send.at[peer, mine_half],
-                dst_ref=packet_all.at[me, mine_half],
-                send_sem=packet_send_sem.at[k],
-                recv_sem=packet_recv_sem.at[k],
-                device_id={"ap": peer},
-                device_id_type=MESH,
-            )
-            copy.start()
-            packets[k] = copy
+            sample_copies[k].wait_recv()
 
     relays = {}
 
@@ -487,9 +496,9 @@
     tiles = tones // LANES
     station_of = lax.broadcasted_iota(jnp.int32, (rows, 1), 0)
 
-    def prepare(origin, packet, signals, slot):
-        high = packet[pieces : pieces + held_rows].reshape(kinds * stations, COARSE)
-        low = packet[pieces + held_rows :].reshape(kinds * stations, COARSE)
+    def prepare(held, signals, slot):
+        high = held[: kinds * stations, :]
+        low = held[kinds * stations :, :]
         cov[slot] = jnp.dot(
             jnp.concatenate([high, high], axis=1),
             spread[...],
@@ -541,7 +550,7 @@
                 solved[slot, i, 2, :, lanes] = re + im
 
     def combine(origin, packet, slot):
-        coefs = packet[:pieces].reshape(pieces * block, 2 * TAPS)
+        coefs = packet[...].reshape(pieces * block, 2 * TAPS)
         for l in range(tiles):
             columns = pl.ds(l * 2 * LANES, 2 * LANES)
             smooth[slot, l] = jnp.dot(coefs, table[:, columns], preferred_element_type=jnp.float32)
@@ -588,15 +597,21 @@
         copy.start()
         share_copies.append(copy)
 
-    tasks = [(me, packet_send.at[me], received_ref, 0)]
+    tasks = [(me, packet_send.at[me], sample_send, received_ref, 0)]
     for step in range(1, steps + 1):
         for direction in range(2 if step <= n - 1 - n // 2 else 1):
             origin = origin_of(direction, step)
-            tasks.append((origin, packet_all.at[origin], signal_all.at[origin], step))
-
-    prepare(*tasks[0][:3], 0)
+            tasks.append(
+                (origin, packet_all.at[origin], sample_all.at[origin], signal_all.at[origin], step)
+            )
+
+    ring_step(0, 1)
+    prepare(*tasks[0][2:4], 0)
     combine(*tasks[0][:2], 0)
     send_share(me)
+    for c in range(1, stations):
+        ring_step(c, 1)
+    relay_start(1)
     for copy in gain_copies:
         copy.wait_recv()
     totals = jnp.zeros((1, users), jnp.float32)
@@ -624,28 +639,39 @@
         copy.start()
         place_copies.append(copy)
 
-    def advance(step, c):
-        if step <= steps:
-            ring_step(c, step)
-
-    relay_start(1)
-    for c in range(stations):
-        advance(2, c)
-    relay_wait(1)
-    prepare(*tasks[1][:3], 1)
+    sample_wait(1)
+    prepare(*tasks[1][2:4], 1)
+    advanced = {0: 1}
+    if steps > 1:
+        ring_step(0, 2)
+        advanced[0] = 2
     for t in range(1, len(tasks)):
-        origin, packet, _, step = tasks[t]
+        origin, packet, _, _, step = tasks[t]
         last = t + 1 == len(tasks)
-        if not last and tasks[t + 1][3] > step:
-            relay_start(step + 1)
+        begins = tasks[t - 1][4] < step
+        after = step if last else tasks[t + 1][4]
+        if begins:
+            relay_wait(step)
+        if after > step:
+            split = after == steps
+            if split:
+                combine(origin, packet, t % 2)
             for c in range(stations):
-                if step + 1 > 2:
-                    advance(step + 1, c)
-            relay_wait(step + 1)
-        combine(origin, packet, t % 2)
+                if advanced.get(c, 1) < after:
+                    ring_step(c, after)
+                    advanced[c] = after
+            sample_wait(after)
+            relay_start(after)
+            if not split:
+                combine(origin, packet, t % 2)
+        else:
+            combine(origin, packet, t % 2)
         if not last:
-            prepare(*tasks[t + 1][:3], (t + 1) % 2)
+            prepare(*tasks[t + 1][2:4], (t + 1) % 2)
         send_share(origin)
+        if begins and not last and step < steps and advanced.get(0, 1) < step + 1:
+            ring_step(0, step + 1)
+            advanced[0] = step + 1
     for copy in share_copies + place_copies:
         copy.wait()
     for copy in relays.values():
@@ -654,7 +680,7 @@
         copy.wait_send()
     for copy in gain_copies:
         copy.wait_send()
-    for copy in packets.values():
+    for copy in list(packets.values()) + list(sample_copies.values()):
         copy.wait_send()
     for copy in ring_copies.values():
         copy.wait_send()
@@ -756,7 +782,7 @@
     pieces = stations * antennas
     block = PEER_MAX * CU
     rows = stations * symbols
-    parcels = pieces + 2 * (antennas * antennas * stations // block)
+    held = 2 * antennas * antennas * stations
     steps = n // 2
     dma = pltpu.SemaphoreType.DMA
     bf16, f32 = jnp.bfloat16, jnp.float32
@@ -773,7 +799,8 @@
         in_specs=[hbm] * 12,
         out_specs=(hbm, hbm, hbm),
         scratch_shapes=[
-            pltpu.VMEM((n, parcels, block, 2 * TAPS), bf16),
+            pltpu.VMEM((n, pieces, block, 2 * TAPS), bf16),
+            pltpu.VMEM((n, held, COARSE), bf16),
             pltpu.VMEM((n,) + received.shape, bf16),
             pltpu.VMEM(received.shape, bf16),
             pltpu.VMEM((1, users), f32),
@@ -789,7 +816,8 @@
             pltpu.VMEM((2 * COARSE, tones), bf16),
             pltpu.VMEM((pieces, users, 2 * TAPS), bf16),
             pltpu.VMEM((pieces, users, 2 * TAPS), bf16),
-            pltpu.VMEM((n, parcels, block, 2 * TAPS), bf16),
+            pltpu.VMEM((n, pieces, block, 2 * TAPS), bf16),
+            pltpu.VMEM((held, COARSE), bf16),
             pltpu.VMEM((pieces * users, 2 * TAPS), bf16),
             pltpu.VMEM((n, stations, users), f32),
             pltpu.VMEM((n * block, users), bf16),
@@ -807,6 +835,8 @@
             dma((4,)),
             dma((pieces,)),
             dma((pieces,)),
+            dma((n,)),
+            dma((n,)),
             dma((n,)),
             dma((n,)),
             dma((n,)),

time: 31.3 us -> 33.9 us (1.083)
  Pallas kernels: 31.2 us -> 33.6 us
    pallas_call x1, Pallas kernels: 27.6 us -> 30 us  [local(): pl.pallas_call(functools.partial(uplink_kernel, n, ring_of), out_shape=(j...]
where the time goes in v4:
time: 33.9 us; the launch traced here: 33.6 us
  Pallas kernels  33.6 us (99%)
    pallas_call x1, Pallas kernels, local(): pl.pallas_call(functools.partial(uplink_kernel, n, ring_of), out_shape=(j...  30 us
    pallas_call x1, Pallas kernels, local(): pl.pallas_call(place_kernel, out_shape=jax.ShapeDtypeStruct((slots, symbo...  3.55 us

profile of v4, /device:TPU:0, one launch (start us, length us, event | category | flops | bytes accessed | tf_op | source)
XLA Modules:
  0.0 33.6 jit_solution(1163188729512984314)
XLA Ops:
  0.0 30.0 %uplink.1 = (bf16[8,128,1024]{2,1,0:T(8,128)(2,1)}, bf16[32,128]{1,0:T(8,128)(2,1)}, f32[32,128]{1,0:T(8,128)}) custom-call(bf16[2,4,2,128,1024]{4,3,2,1,0:T(8,128)(2,1)} %guess_hbm.1, bf16[2,4,2,4,1024]{4,3,2,1,0:T(4,128)(2,1)} %received_hbm.1, f32[1,128]{1,0:T(1,128)} %bitcast.9, f32[1,2]{1,0:T(1,128)} %bitcast.10, f32[2,128]{1,0:T(2,128)} %gain_hbm.1, ...), custom_call_target="tpu_custom_call" | custom-call | tf_op jit(solution)/shard_map/uplink/pallas_call | solution.py:792
  30.0 3.6 %place.1 = f32[32,4,16,128]{3,2,1,0:T(8,128)} custom-call(bf16[32,128]{1,0:T(8,128)(2,1)} %get-tuple-element.8.place_hbm, f32[32,128]{1,0:T(8,128)} %get-tuple-element.9.scale_hbm, bf16[8,128,1024]{2,1,0:T(8,128)(2,1)} %get-tuple-element.10.share_hbm), custom_call_target="tpu_custom_call" | custom-call | tf_op jit(solution)/shard_map/place/pallas_call | solution.py:870

commit v5 on v3

--- a/solution.py
+++ b/solution.py
@@ -226,6 +226,7 @@
     relay_recv_sem,
     share_sem,
     place_sem,
+    present,
 ):
     stations, antennas, _, users, tones = guess.shape
     pieces = stations * antennas
@@ -250,21 +251,33 @@
         )
     received_copy = pltpu.make_async_copy(received_hbm, received_ref, place_sem.at[0])
     received_copy.start()
-    table_copies[0].start()
+    small_copies = []
+    for source, into in (
+        (cluster_hbm, cluster_ref),
+        (serving_hbm, serving_ref),
+        (owner_hbm, owner_ref),
+        (power_hbm, power_ref),
+        (gain_hbm, gain_ref),
+        (noise_hbm, noise_ref),
+    ):
+        copy = pltpu.make_async_copy(source, into, small_sem.at[len(small_copies)])
+        copy.start()
+        small_copies.append(copy)
     guess_copies = []
     for q in range(pieces):
         a, i = q // antennas, q % antennas
         copy = pltpu.make_async_copy(guess_hbm.at[a, i], guess.at[a, i], guess_sem.at[q])
         guess_copies.append(copy)
-    for copy in guess_copies[: pieces // 2]:
-        copy.start()
+
     barrier = pltpu.get_barrier_semaphore()
     pl.semaphore_signal(barrier, inc=1, device_id={"sc": 1 - part}, device_id_type=MESH)
-    for k in range(1, n):
-        pl.semaphore_signal(
-            barrier, inc=1, device_id={"ap": lax.rem(me + k, n)}, device_id_type=MESH
-        )
-
+    for peer in (left, right):
+        pl.semaphore_signal(barrier, inc=1, device_id={"ap": peer}, device_id_type=MESH)
+    table_copies[0].start()
+    for copy in guess_copies:
+        copy.start()
+    for copy in table_copies[1:]:
+        copy.start()
     ring_copies = {}
     reach = {}
     for c in range(stations):
@@ -298,75 +311,27 @@
             copy.start()
             ring_copies[c, direction, step] = copy
 
-    table_copies[0].wait()
-    for copy in guess_copies[pieces // 2 :]:
-        copy.start()
-    small_copies = []
-    for source, into in (
-        (cluster_hbm, cluster_ref),
-        (serving_hbm, serving_ref),
-        (owner_hbm, owner_ref),
-        (power_hbm, power_ref),
-        (gain_hbm, gain_ref),
-        (noise_hbm, noise_ref),
-    ):
-        copy = pltpu.make_async_copy(source, into, small_sem.at[len(small_copies)])
-        copy.start()
-        small_copies.append(copy)
-    for copy in table_copies[1:]:
-        copy.start()
-
-    half_copies = []
-    together = 2
-    lower = lax.broadcasted_iota(jnp.int32, (users, 2 * TAPS), 1) < TAPS
-    for first in range(0, pieces, together):
-        group = range(first, first + together)
-        for q in group:
-            guess_copies[q].wait()
-        a, i = first // antennas, first % antennas
-        products = jnp.dot(
-            guess[a, i : i + together].reshape(together * 2 * users, tones),
-            taps[...],
-            preferred_element_type=jnp.float32,
-        )
-        for q in group:
-            at = (q - first) * 2 * users
-            turned = pltpu.roll(products[at + users : at + 2 * users], TAPS, axis=1)
-            sums = products[at : at + users] + jnp.where(lower, -turned, turned)
-            half[q] = (sums * (1.0 / TONE_NUMBER)).astype(jnp.bfloat16)
-        if first == 0:
-            pl.semaphore_wait(barrier, n)
-            received_copy.wait()
-            for c in range(stations):
-                ring_step(c, 0)
-        for q in group:
-            copy = pltpu.make_async_remote_copy(
-                src_ref=half.at[q],
-                dst_ref=other.at[q],
-                send_sem=half_send_sem.at[q],
-                recv_sem=half_recv_sem.at[q],
-                device_id={"sc": 1 - part},
-                device_id_type=MESH,
-            )
-            copy.start()
-            half_copies.append(copy)
-
+    received_copy.wait()
     for copy in small_copies:
         copy.wait()
-    gain_copies = []
-    for k in range(1, n):
-        peer = lax.rem(me + k, n)
-        copy = pltpu.make_async_remote_copy(
-            src_ref=gain_ref,
-            dst_ref=gains.at[me],
-            send_sem=gain_send_sem.at[k],
-            recv_sem=gain_recv_sem.at[n - k],
-            device_id={"ap": peer},
-            device_id_type=MESH,
-        )
-        copy.start()
-        gain_copies.append(copy)
-    gains[me] = gain_ref[...]
+
+    def present_send(level):
+        if level < steps:
+            for side, peer in ((0, right), (1, left)):
+                pl.semaphore_signal(
+                    present.at[side, level], inc=1, device_id={"ap": peer}, device_id_type=MESH
+                )
+
+    def present_wait(level):
+        if level < steps:
+            for side in range(2):
+                pl.semaphore_wait(present.at[side, level], 1)
+            present_send(level + 1)
+
+    pl.semaphore_wait(barrier, 3)
+    present_send(1)
+    for c in range(stations):
+        ring_step(c, 0)
     owner_u, rank_u, served_u, before_u, serve_u, position = user_tables(
         cluster_ref[...], serving_ref[...], owner_ref[...], clusters, users, stations, n
     )
@@ -388,25 +353,58 @@
     wide = jnp.broadcast_to(power_ref[...] * (1.0 / users), (LANES, users))
     power_wide[...] = jnp.transpose(wide)
 
-    ring_step(0, 1)
+    present_wait(1)
+    table_copies[0].wait()
+    for copy in guess_copies:
+        copy.wait()
+    count = pieces * users
+    lower = lax.broadcasted_iota(jnp.int32, (count, 2 * TAPS), 1) < TAPS
+    products = [
+        jnp.dot(
+            guess[:, :, reim].reshape(count, tones), taps[...], preferred_element_type=jnp.float32
+        )
+        for reim in range(2)
+    ]
+    turned = pltpu.roll(products[1], TAPS, axis=1)
+    sums = products[0] + jnp.where(lower, -turned, turned)
+    half[...] = (sums * (1.0 / TONE_NUMBER)).astype(jnp.bfloat16).reshape(half.shape)
+    present_wait(2)
+    half_copies = []
+    for q in range(pieces):
+        copy = pltpu.make_async_remote_copy(
+            src_ref=half.at[q],
+            dst_ref=other.at[q],
+            send_sem=half_send_sem.at[q],
+            recv_sem=half_recv_sem.at[q],
+            device_id={"sc": 1 - part},
+            device_id_type=MESH,
+        )
+        copy.start()
+        half_copies.append(copy)
+    sums = []
     for q in range(pieces):
         half_copies[q].wait_recv()
         total = (half[q].astype(jnp.float32) + other[q].astype(jnp.float32)).astype(jnp.bfloat16)
         coef_b[pl.ds(q * users, users), :] = total
-        chosen = jnp.dot(pick[...], total, preferred_element_type=jnp.float32)
-        chosen = chosen * pick_weight[q // antennas]
-        packet_send[:, q] = chosen.astype(jnp.bfloat16).reshape(n, block, 2 * TAPS)
+        sums.append(total)
     symbols = received_ref.shape[3]
     rows = stations * symbols
     entries = [(i, j) for i in range(antennas) for j in range(i + 1)]
     kinds = antennas * antennas
-    for c in range(1, stations):
-        ring_step(c, 1)
+    ring_step(0, 1)
     for copy in table_copies[1:]:
         copy.wait()
     both = jnp.dot(coef_b[...], coarse[...], preferred_element_type=jnp.float32)
     for reim in range(2):
         sampled[reim] = both[:, reim * COARSE : (reim + 1) * COARSE]
+    chosen = jnp.dot(
+        pick[...], jnp.concatenate(sums, axis=1), preferred_element_type=jnp.float32
+    )
+    for q in range(pieces):
+        values = chosen[:, q * 2 * TAPS : (q + 1) * 2 * TAPS] * pick_weight[q // antennas]
+        packet_send[:, q] = values.astype(jnp.bfloat16).reshape(n, block, 2 * TAPS)
+    for c in range(1, stations):
+        ring_step(c, 1)
     for a in range(stations):
 
         def body(step, sums, a=a):
@@ -449,12 +447,14 @@
     parcels = packet_send.shape[1]
     mine_half = pl.ds(part * (parcels // 2), parcels // 2)
     packets = {}
-    for step in range(1, steps + 1):
+
+    def packet_start(step):
+        window = mine_half
         for k in sorted({step, n - step}):
             peer = node(lax.rem(spot + k, n))
             copy = pltpu.make_async_remote_copy(
-                src_ref=packet_send.at[peer, mine_half],
-                dst_ref=packet_all.at[me, mine_half],
+                src_ref=packet_send.at[peer, window],
+                dst_ref=packet_all.at[me, window],
                 send_sem=packet_send_sem.at[k],
                 recv_sem=packet_recv_sem.at[k],
                 device_id={"ap": peer},
@@ -463,6 +463,24 @@
             copy.start()
             packets[k] = copy
 
+    for level in range(3, steps):
+        present_wait(level)
+    for step in range(1, steps + 1):
+        packet_start(step)
+    gain_copies = []
+    for k in range(1, n):
+        peer = lax.rem(me + k, n)
+        copy = pltpu.make_async_remote_copy(
+            src_ref=gain_ref,
+            dst_ref=gains.at[me],
+            send_sem=gain_send_sem.at[k],
+            recv_sem=gain_recv_sem.at[n - k],
+            device_id={"ap": peer},
+            device_id_type=MESH,
+        )
+        copy.start()
+        gain_copies.append(copy)
+    gains[me] = gain_ref[...]
     relays = {}
 
     def relay_start(step):
@@ -487,7 +505,7 @@
     tiles = tones // LANES
     station_of = lax.broadcasted_iota(jnp.int32, (rows, 1), 0)
 
-    def prepare(origin, packet, signals, slot):
+    def prepare(packet, signals, slot):
         high = packet[pieces : pieces + held_rows].reshape(kinds * stations, COARSE)
         low = packet[pieces + held_rows :].reshape(kinds * stations, COARSE)
         cov[slot] = jnp.dot(
@@ -594,58 +612,70 @@
             origin = origin_of(direction, step)
             tasks.append((origin, packet_all.at[origin], signal_all.at[origin], step))
 
-    prepare(*tasks[0][:3], 0)
+    prepare(*tasks[0][1:3], 0)
     combine(*tasks[0][:2], 0)
     send_share(me)
-    for copy in gain_copies:
-        copy.wait_recv()
-    totals = jnp.zeros((1, users), jnp.float32)
-    for p in range(n):
-        for a in range(stations):
-            row = serve_u[p * stations + a : p * stations + a + 1] * gains[p, a : a + 1, :]
-            totals = totals + row
-    scale = 1.0 / (1.0 + totals)
-    held = owner_u == mef
-    slot_user = iota((OWN_MAX * CU, users), 0) == jnp.where(held, rank_u * CU + position, -1.0)
-    slot_rows = jnp.where(slot_user, 1.0, 0.0)
-    slot_scale = jnp.sum(jnp.where(slot_user, scale, 0.0), axis=1, keepdims=True)
-    scale_ref[...] = jnp.broadcast_to(slot_scale, (OWN_MAX * CU, LANES))
-    hits = []
-    for p in range(n):
-        goal = jnp.where(
-            held & (served_u[p : p + 1] > 0.5), before_u[p : p + 1] * CU + position, -1.0
-        )
-        hits.append(jnp.where(iota((block, users), 0) == goal, 1.0, 0.0))
-    placement = exact_dot(slot_rows, jnp.concatenate(hits, axis=0), ((1,), (1,)))
-    place_ref[...] = placement.astype(jnp.bfloat16)
-    place_copies = []
-    for source, into in ((place_ref, place_hbm), (scale_ref, scale_hbm)):
-        copy = pltpu.make_async_copy(source, into, place_sem.at[1 + len(place_copies)])
-        copy.start()
-        place_copies.append(copy)
-
-    def advance(step, c):
-        if step <= steps:
+    if steps > 1:
+        ring_step(0, 2)
+    relay_start(1)
+    relay_wait(1)
+    prepare(*tasks[1][1:3], 1)
+    advanced = {(c, 1) for c in range(stations)} | {(0, 2)}
+
+    def advance(c, step):
+        if step <= steps and (c, step) not in advanced:
             ring_step(c, step)
-
-    relay_start(1)
-    for c in range(stations):
-        advance(2, c)
-    relay_wait(1)
-    prepare(*tasks[1][:3], 1)
+            advanced.add((c, step))
+
+    for c in range(1, stations):
+        advance(c, 2)
     for t in range(1, len(tasks)):
         origin, packet, _, step = tasks[t]
         last = t + 1 == len(tasks)
-        if not last and tasks[t + 1][3] > step:
-            relay_start(step + 1)
-            for c in range(stations):
-                if step + 1 > 2:
-                    advance(step + 1, c)
-            relay_wait(step + 1)
+        after = step if last else tasks[t + 1][3]
+        begins = tasks[t - 1][3] < step
         combine(origin, packet, t % 2)
         if not last:
-            prepare(*tasks[t + 1][:3], (t + 1) % 2)
+            if after > step:
+                for c in range(stations):
+                    advance(c, after)
+                relay_wait(after)
+            prepare(*tasks[t + 1][1:3], (t + 1) % 2)
         send_share(origin)
+        if begins and step < steps:
+            advance(0, step + 1)
+            if step == 1:
+                for c in range(1, stations):
+                    advance(c, 2)
+            relay_start(step + 1)
+        if t == len(tasks) - 3:
+            for copy in gain_copies:
+                copy.wait_recv()
+            totals = jnp.zeros((1, users), jnp.float32)
+            for p in range(n):
+                for a in range(stations):
+                    row = serve_u[p * stations + a : p * stations + a + 1] * gains[p, a : a + 1, :]
+                    totals = totals + row
+            scale = 1.0 / (1.0 + totals)
+            held = owner_u == mef
+            slot_user = iota((OWN_MAX * CU, users), 0) == jnp.where(held, rank_u * CU + position, -1.0)
+            slot_rows = jnp.where(slot_user, 1.0, 0.0)
+            slot_scale = jnp.sum(jnp.where(slot_user, scale, 0.0), axis=1, keepdims=True)
+            scale_ref[...] = jnp.broadcast_to(slot_scale, (OWN_MAX * CU, LANES))
+            hits = []
+            for p in range(n):
+                goal = jnp.where(
+                    held & (served_u[p : p + 1] > 0.5), before_u[p : p + 1] * CU + position, -1.0
+                )
+                hits.append(jnp.where(iota((block, users), 0) == goal, 1.0, 0.0))
+            placement = exact_dot(slot_rows, jnp.concatenate(hits, axis=0), ((1,), (1,)))
+            place_ref[...] = placement.astype(jnp.bfloat16)
+            place_copies = []
+            for source, into in ((place_ref, place_hbm), (scale_ref, scale_hbm)):
+                copy = pltpu.make_async_copy(source, into, place_sem.at[1 + len(place_copies)])
+                copy.start()
+                place_copies.append(copy)
+
     for copy in share_copies + place_copies:
         copy.wait()
     for copy in relays.values():
@@ -664,35 +694,41 @@
     place_hbm, scale_hbm, share_hbm, out_hbm, place_ref, scale_ref, share, lines, small_sem, in_sem, out_sem
 ):
     kinds, _, tones = share.shape
+    symbols, tiles = kinds // 2, tones // LANES
+    arrivals = []
+    for kind in range(kinds):
+        arrivals.append(
+            pltpu.make_async_copy(share_hbm.at[kind], share.at[kind], in_sem.at[kind])
+        )
     smalls = []
     for source, into in ((place_hbm, place_ref), (scale_hbm, scale_ref)):
         copy = pltpu.make_async_copy(source, into, small_sem.at[len(smalls)])
         copy.start()
         smalls.append(copy)
-    symbols, tiles = kinds // 2, tones // LANES
-    arrivals = []
-    for kind in range(kinds):
-        copy = pltpu.make_async_copy(share_hbm.at[kind], share.at[kind], in_sem.at[kind])
+    for copy in arrivals:
         copy.start()
-        arrivals.append(copy)
     for copy in smalls:
         copy.wait()
     copies = []
     for s in range(symbols):
+        placed = []
         for reim in range(2):
             arrivals[s * 2 + reim].wait()
-            placed = jnp.dot(
-                place_ref[...], share[s * 2 + reim], preferred_element_type=jnp.float32
+            placed.append(
+                jnp.dot(place_ref[...], share[s * 2 + reim], preferred_element_type=jnp.float32)
             )
-            for l in range(tiles):
-                for r in range(OWN_MAX):
-                    rows = slice(r * CU, (r + 1) * CU)
-                    value = placed[rows, l * LANES : (l + 1) * LANES] * scale_ref[rows]
-                    lines[s, pl.ds(r * CU * 2 * tiles + l * 2 + reim, CU, stride=2 * tiles), :] = value
-        height = 2 * tiles
-        copy = pltpu.make_async_copy(
-            lines.at[s].reshape(OWN_MAX * CU, height, LANES), out_hbm.at[:, s], out_sem.at[s]
-        )
+        for r in range(OWN_MAX):
+            rows = slice(r * CU, (r + 1) * CU)
+            scale = scale_ref[rows]
+            parts = [
+                placed[reim][rows, l * LANES : (l + 1) * LANES] * scale
+                for l in range(tiles)
+                for reim in range(2)
+            ]
+            for first in range(0, 2 * tiles, CU):
+                square = jnp.stack(parts[first : first + CU], axis=0)
+                lines[s, rows, first : first + CU, :] = jnp.transpose(square, (1, 0, 2))
+        copy = pltpu.make_async_copy(lines.at[s], out_hbm.at[:, s], out_sem.at[s])
         copy.start()
         copies.append(copy)
     for copy in copies:
@@ -818,6 +854,7 @@
             dma((n,)),
             dma((n,)),
             dma((3,)),
+            pltpu.SemaphoreType.REGULAR((2, steps)),
         ],
         compiler_params=pltpu.CompilerParams(
             collective_id=0, has_side_effects=True, vmem_limit_bytes=VMEM_BYTES
@@ -846,7 +883,7 @@
             pltpu.VMEM((slots, n * block), bf16),
             pltpu.VMEM((slots, LANES), f32),
             pltpu.VMEM((symbols * 2, n * block, tones), bf16),
-            pltpu.VMEM((symbols, slots * tiles * 2, LANES), f32),
+            pltpu.VMEM((symbols, slots, tiles * 2, LANES), f32),
             dma((2,)),
             dma((symbols * 2,)),
             dma((symbols,)),

time: 31.3 us -> 30.5 us (0.974)
  Pallas kernels: 31.2 us -> 30.4 us
    pallas_call x1, Pallas kernels: 27.6 us -> 26.8 us  [local(): pl.pallas_call(functools.partial(uplink_kernel, n, ring_of), out_shape=(j...]
where the time goes in v5:
time: 30.5 us; the launch traced here: 30.4 us
  Pallas kernels  30.4 us (100%)
    pallas_call x1, Pallas kernels, local(): pl.pallas_call(functools.partial(uplink_kernel, n, ring_of), out_shape=(j...  26.8 us
    pallas_call x1, Pallas kernels, local(): pl.pallas_call(place_kernel, out_shape=jax.ShapeDtypeStruct((slots, symbo...  3.54 us

profile of v5, /device:TPU:0, one launch (start us, length us, event | category | flops | bytes accessed | tf_op | source)
XLA Modules:
  0.0 30.4 jit_solution(14484642915959550947)
XLA Ops:
  0.0 26.8 %uplink.1 = (bf16[8,128,1024]{2,1,0:T(8,128)(2,1)}, bf16[32,128]{1,0:T(8,128)(2,1)}, f32[32,128]{1,0:T(8,128)}) custom-call(bf16[2,4,2,128,1024]{4,3,2,1,0:T(8,128)(2,1)} %guess_hbm.1, bf16[2,4,2,4,1024]{4,3,2,1,0:T(4,128)(2,1)} %received_hbm.1, f32[1,128]{1,0:T(1,128)} %bitcast.9, f32[1,2]{1,0:T(1,128)} %bitcast.10, f32[2,128]{1,0:T(2,128)} %gain_hbm.1, ...), custom_call_target="tpu_custom_call" | custom-call | tf_op jit(solution)/shard_map/uplink/pallas_call | solution.py:802
  26.8 3.5 %place.1 = f32[32,4,16,128]{3,2,1,0:T(8,128)} custom-call(bf16[32,128]{1,0:T(8,128)(2,1)} %get-tuple-element.8.place_hbm, f32[32,128]{1,0:T(8,128)} %get-tuple-element.9.scale_hbm, bf16[8,128,1024]{2,1,0:T(8,128)(2,1)} %get-tuple-element.10.share_hbm), custom_call_target="tpu_custom_call" | custom-call | tf_op jit(solution)/shard_map/place/pallas_call | solution.py:877

commit v6 on v5

--- a/solution.py
+++ b/solution.py
@@ -266,7 +266,7 @@
     guess_copies = []
     for q in range(pieces):
         a, i = q // antennas, q % antennas
-        copy = pltpu.make_async_copy(guess_hbm.at[a, i], guess.at[a, i], guess_sem.at[q])
+        copy = pltpu.make_async_copy(guess_hbm.at[a, i], guess.at[a, i], guess_sem)
         guess_copies.append(copy)
 
     barrier = pltpu.get_barrier_semaphore()
@@ -280,36 +280,42 @@
         copy.start()
     ring_copies = {}
     reach = {}
-    for c in range(stations):
+    fine = 2 * stations
+    for c in range(fine):
         far, near = n // 2, n - 1 - n // 2
         reach[c] = (far, near) if c % 2 == 0 else (near, far)
     steps = max(max(r) for r in reach.values())
 
+    def fine_part(ref, c):
+        some = antennas // 2
+        return ref.at[c // 2, pl.ds(c % 2 * some, some)]
+
     def origin_of(direction, step):
         back = lax.rem(spot + n - step, n) if direction == 0 else lax.rem(spot + step, n)
         return node(back)
 
-    def ring_step(c, step):
-        for direction in range(2):
-            if step > reach[c][direction]:
-                continue
-            origin = origin_of(direction, step)
-            source = received_ref.at[c]
-            if step > 0:
-                ring_copies[c, direction, step - 1].wait_recv()
-                source = signal_all.at[origin, c]
-            if step == reach[c][direction]:
-                continue
-            copy = pltpu.make_async_remote_copy(
-                src_ref=source,
-                dst_ref=signal_all.at[origin, c],
-                send_sem=ring_send_sem.at[direction, c, step],
-                recv_sem=ring_recv_sem.at[direction, c, step],
-                device_id={"ap": right if direction == 0 else left},
-                device_id_type=MESH,
-            )
-            copy.start()
-            ring_copies[c, direction, step] = copy
+    def ring_step(a, step):
+        for c in range(a * fine // stations, (a + 1) * fine // stations):
+            for direction in range(2):
+                if step > reach[c][direction]:
+                    continue
+                origin = origin_of(direction, step)
+                source = fine_part(received_ref, c)
+                if step > 0:
+                    ring_copies[c, direction, step - 1].wait_recv()
+                    source = fine_part(signal_all.at[origin], c)
+                if step == reach[c][direction]:
+                    continue
+                copy = pltpu.make_async_remote_copy(
+                    src_ref=source,
+                    dst_ref=fine_part(signal_all.at[origin], c),
+                    send_sem=ring_send_sem,
+                    recv_sem=ring_recv_sem.at[direction, c, step],
+                    device_id={"ap": right if direction == 0 else left},
+                    device_id_type=MESH,
+                )
+                copy.start()
+                ring_copies[c, direction, step] = copy
 
     received_copy.wait()
     for copy in small_copies:
@@ -355,8 +361,7 @@
 
     present_wait(1)
     table_copies[0].wait()
-    for copy in guess_copies:
-        copy.wait()
+    pltpu.make_async_copy(guess_hbm, guess, guess_sem).wait()
     count = pieces * users
     lower = lax.broadcasted_iota(jnp.int32, (count, 2 * TAPS), 1) < TAPS
     products = [
@@ -370,20 +375,23 @@
     half[...] = (sums * (1.0 / TONE_NUMBER)).astype(jnp.bfloat16).reshape(half.shape)
     present_wait(2)
     half_copies = []
-    for q in range(pieces):
+    for a in range(stations):
+        window = pl.ds(a * antennas, antennas)
         copy = pltpu.make_async_remote_copy(
-            src_ref=half.at[q],
-            dst_ref=other.at[q],
-            send_sem=half_send_sem.at[q],
-            recv_sem=half_recv_sem.at[q],
+            src_ref=half.at[window],
+            dst_ref=other.at[window],
+            send_sem=half_send_sem.at[a],
+            recv_sem=half_recv_sem.at[a],
             device_id={"sc": 1 - part},
             device_id_type=MESH,
         )
         copy.start()
         half_copies.append(copy)
+    ring_step(0, 1)
     sums = []
     for q in range(pieces):
-        half_copies[q].wait_recv()
+        if q % antennas == 0:
+            half_copies[q // antennas].wait_recv()
         total = (half[q].astype(jnp.float32) + other[q].astype(jnp.float32)).astype(jnp.bfloat16)
         coef_b[pl.ds(q * users, users), :] = total
         sums.append(total)
@@ -391,7 +399,6 @@
     rows = stations * symbols
     entries = [(i, j) for i in range(antennas) for j in range(i + 1)]
     kinds = antennas * antennas
-    ring_step(0, 1)
     for copy in table_copies[1:]:
         copy.wait()
     both = jnp.dot(coef_b[...], coarse[...], preferred_element_type=jnp.float32)
@@ -455,7 +462,7 @@
             copy = pltpu.make_async_remote_copy(
                 src_ref=packet_send.at[peer, window],
                 dst_ref=packet_all.at[me, window],
-                send_sem=packet_send_sem.at[k],
+                send_sem=packet_send_sem,
                 recv_sem=packet_recv_sem.at[k],
                 device_id={"ap": peer},
                 device_id_type=MESH,
@@ -467,19 +474,28 @@
         present_wait(level)
     for step in range(1, steps + 1):
         packet_start(step)
-    gain_copies = []
+
+    def gain_all():
+        return pltpu.make_async_remote_copy(
+            src_ref=gains.at[pl.ds(0, n - 1)],
+            dst_ref=gains.at[pl.ds(0, n - 1)],
+            send_sem=gain_send_sem,
+            recv_sem=gain_recv_sem,
+            device_id={"ap": right},
+            device_id_type=MESH,
+        )
+
     for k in range(1, n):
         peer = lax.rem(me + k, n)
         copy = pltpu.make_async_remote_copy(
             src_ref=gain_ref,
             dst_ref=gains.at[me],
-            send_sem=gain_send_sem.at[k],
-            recv_sem=gain_recv_sem.at[n - k],
+            send_sem=gain_send_sem,
+            recv_sem=gain_recv_sem,
             device_id={"ap": peer},
             device_id_type=MESH,
         )
         copy.start()
-        gain_copies.append(copy)
     gains[me] = gain_ref[...]
     relays = {}
 
@@ -490,7 +506,7 @@
             copy = pltpu.make_async_remote_copy(
                 src_ref=packet_all.at[origin, mine_half],
                 dst_ref=packet_all.at[origin, mine_half],
-                send_sem=relay_send_sem.at[k],
+                send_sem=relay_send_sem,
                 recv_sem=relay_recv_sem.at[k],
                 device_id={"sc": 1 - part},
                 device_id_type=MESH,
@@ -596,15 +612,12 @@
                         jnp.bfloat16
                     )
 
-    share_copies = []
-
     def send_share(origin):
         here = pl.ds(pl.multiple_of(origin * block, block), block)
         copy = pltpu.make_async_copy(
-            share.at[:, here], share_hbm.at[:, here], share_sem.at[len(share_copies)]
+            share.at[:, here], share_hbm.at[:, here], share_sem
         )
         copy.start()
-        share_copies.append(copy)
 
     tasks = [(me, packet_send.at[me], received_ref, 0)]
     for step in range(1, steps + 1):
@@ -649,8 +662,7 @@
                     advance(c, 2)
             relay_start(step + 1)
         if t == len(tasks) - 3:
-            for copy in gain_copies:
-                copy.wait_recv()
+            gain_all().wait_recv()
             totals = jnp.zeros((1, users), jnp.float32)
             for p in range(n):
                 for a in range(stations):
@@ -676,18 +688,29 @@
                 copy.start()
                 place_copies.append(copy)
 
-    for copy in share_copies + place_copies:
+    pltpu.make_async_copy(share, share_hbm, share_sem).wait()
+    for copy in place_copies:
         copy.wait()
-    for copy in relays.values():
-        copy.wait_send()
     for copy in half_copies:
         copy.wait_send()
-    for copy in gain_copies:
-        copy.wait_send()
-    for copy in packets.values():
-        copy.wait_send()
-    for copy in ring_copies.values():
-        copy.wait_send()
+    gain_all().wait_send()
+    for send_sem in (packet_send_sem, relay_send_sem):
+        pltpu.make_async_remote_copy(
+            src_ref=packet_all.at[pl.ds(0, n - 1), mine_half],
+            dst_ref=packet_all.at[pl.ds(0, n - 1), mine_half],
+            send_sem=send_sem,
+            recv_sem=packet_recv_sem.at[0],
+            device_id={"ap": right},
+            device_id_type=MESH,
+        ).wait_send()
+    pltpu.make_async_remote_copy(
+        src_ref=signal_all.at[pl.ds(0, n - 1)],
+        dst_ref=signal_all.at[pl.ds(0, n - 1)],
+        send_sem=ring_send_sem,
+        recv_sem=ring_recv_sem.at[0, 0, 0],
+        device_id={"ap": right},
+        device_id_type=MESH,
+    ).wait_send()
 
 
 def place_kernel(
@@ -839,20 +862,20 @@
             pltpu.VMEM((symbols * 2, n * block, tones), bf16),
             pltpu.VMEM((slots, n * block), bf16),
             pltpu.VMEM((slots, LANES), f32),
-            dma((pieces,)),
+            dma,
             dma((4,)),
-            dma((pieces,)),
-            dma((pieces,)),
+            dma((stations,)),
+            dma((stations,)),
+            dma,
+            dma,
+            dma,
             dma((n,)),
+            dma,
+            dma((2, 2 * stations, steps)),
+            dma((6,)),
+            dma,
             dma((n,)),
-            dma((n,)),
-            dma((n,)),
-            dma((2, stations, steps)),
-            dma((2, stations, steps)),
-            dma((6,)),
-            dma((n,)),
-            dma((n,)),
-            dma((n,)),
+            dma,
             dma((3,)),
             pltpu.SemaphoreType.REGULAR((2, steps)),
         ],

time: 30.5 us -> 28.9 us (0.948)
  Pallas kernels: 30.4 us -> 28.7 us
    pallas_call x1, Pallas kernels: 26.8 us -> 25.2 us  [local(): pl.pallas_call(functools.partial(uplink_kernel, n, ring_of), out_shape=(j...]
where the time goes in v6:
time: 28.9 us; the launch traced here: 28.7 us
  Pallas kernels  28.7 us (99%)
    pallas_call x1, Pallas kernels, local(): pl.pallas_call(functools.partial(uplink_kernel, n, ring_of), out_shape=(j...  25.2 us
    pallas_call x1, Pallas kernels, local(): pl.pallas_call(place_kernel, out_shape=jax.ShapeDtypeStruct((slots, symbo...  3.54 us

profile of v6, /device:TPU:0, one launch (start us, length us, event | category | flops | bytes accessed | tf_op | source)
XLA Modules:
  0.0 28.7 jit_solution(14928104683904466064)
XLA Ops:
  0.0 25.2 %uplink.1 = (bf16[8,128,1024]{2,1,0:T(8,128)(2,1)}, bf16[32,128]{1,0:T(8,128)(2,1)}, f32[32,128]{1,0:T(8,128)}) custom-call(bf16[2,4,2,128,1024]{4,3,2,1,0:T(8,128)(2,1)} %guess_hbm.1, bf16[2,4,2,4,1024]{4,3,2,1,0:T(4,128)(2,1)} %received_hbm.1, f32[1,128]{1,0:T(1,128)} %bitcast.9, f32[1,2]{1,0:T(1,128)} %bitcast.10, f32[2,128]{1,0:T(2,128)} %gain_hbm.1, ...), custom_call_target="tpu_custom_call" | custom-call | tf_op jit(solution)/shard_map/uplink/pallas_call | solution.py:825
  25.2 3.5 %place.1 = f32[32,4,16,128]{3,2,1,0:T(8,128)} custom-call(bf16[32,128]{1,0:T(8,128)(2,1)} %get-tuple-element.8.place_hbm, f32[32,128]{1,0:T(8,128)} %get-tuple-element.9.scale_hbm, bf16[8,128,1024]{2,1,0:T(8,128)(2,1)} %get-tuple-element.10.share_hbm), custom_call_target="tpu_custom_call" | custom-call | tf_op jit(solution)/shard_map/place/pallas_call | solution.py:900

commit v7 on v6

--- a/solution.py
+++ b/solution.py
@@ -521,7 +521,7 @@
     tiles = tones // LANES
     station_of = lax.broadcasted_iota(jnp.int32, (rows, 1), 0)
 
-    def prepare(packet, signals, slot):
+    def spread_out(packet, slot):
         high = packet[pieces : pieces + held_rows].reshape(kinds * stations, COARSE)
         low = packet[pieces + held_rows :].reshape(kinds * stations, COARSE)
         cov[slot] = jnp.dot(
@@ -529,6 +529,8 @@
             spread[...],
             preferred_element_type=jnp.float32,
         ) + jnp.dot(low, spread[:COARSE, :], preferred_element_type=jnp.float32)
+
+    def solve(signals, slot):
         width = min(tones, 4 * LANES)
         for base in range(0, tones, width):
             lanes = slice(base, base + width)
@@ -573,6 +575,10 @@
                 solved[slot, i, 0, :, lanes] = re
                 solved[slot, i, 1, :, lanes] = im
                 solved[slot, i, 2, :, lanes] = re + im
+
+    def prepare(packet, signals, slot):
+        spread_out(packet, slot)
+        solve(signals, slot)
 
     def combine(origin, packet, slot):
         coefs = packet[:pieces].reshape(pieces * block, 2 * TAPS)
@@ -642,25 +648,37 @@
 
     for c in range(1, stations):
         advance(c, 2)
+    if steps > 1:
+        relay_start(2)
     for t in range(1, len(tasks)):
         origin, packet, _, step = tasks[t]
         last = t + 1 == len(tasks)
         after = step if last else tasks[t + 1][3]
         begins = tasks[t - 1][3] < step
+        if after == steps > step:
+            relay_wait(after)
         combine(origin, packet, t % 2)
         if not last:
-            if after > step:
+            _, following, signals, _ = tasks[t + 1]
+            if after == steps > step:
+                spread_out(following, (t + 1) % 2)
                 for c in range(stations):
                     advance(c, after)
-                relay_wait(after)
-            prepare(*tasks[t + 1][1:3], (t + 1) % 2)
+                solve(signals, (t + 1) % 2)
+            else:
+                if after > step:
+                    for c in range(stations):
+                        advance(c, after)
+                    relay_wait(after)
+                prepare(following, signals, (t + 1) % 2)
         send_share(origin)
+        if step < after < steps:
+            relay_start(after + 1)
         if begins and step < steps:
             advance(0, step + 1)
             if step == 1:
                 for c in range(1, stations):
                     advance(c, 2)
-            relay_start(step + 1)
         if t == len(tasks) - 3:
             gain_all().wait_recv()
             totals = jnp.zeros((1, users), jnp.float32)
@@ -732,14 +750,14 @@
         copy.start()
     for copy in smalls:
         copy.wait()
+    for copy in arrivals:
+        copy.wait()
     copies = []
     for s in range(symbols):
-        placed = []
-        for reim in range(2):
-            arrivals[s * 2 + reim].wait()
-            placed.append(
-                jnp.dot(place_ref[...], share[s * 2 + reim], preferred_element_type=jnp.float32)
-            )
+        placed = [
+            jnp.dot(place_ref[...], share[s * 2 + reim], preferred_element_type=jnp.float32)
+            for reim in range(2)
+        ]
         for r in range(OWN_MAX):
             rows = slice(r * CU, (r + 1) * CU)
             scale = scale_ref[rows]

time: 28.9 us -> 28 us (0.969)
  Pallas kernels: 28.7 us -> 27.9 us
    pallas_call x1, Pallas kernels: 3.54 us -> 2.85 us  [local(): pl.pallas_call(place_kernel, out_shape=jax.ShapeDtypeStruct((slots, symbo...]
where the time goes in v7:
time: 28 us; the launch traced here: 27.9 us
  Pallas kernels  27.9 us (100%)
    pallas_call x1, Pallas kernels, local(): pl.pallas_call(functools.partial(uplink_kernel, n, ring_of), out_shape=(j...  25 us
    pallas_call x1, Pallas kernels, local(): pl.pallas_call(place_kernel, out_shape=jax.ShapeDtypeStruct((slots, symbo...  2.85 us

profile of v7, /device:TPU:0, one launch (start us, length us, event | category | flops | bytes accessed | tf_op | source)
XLA Modules:
  0.0 27.9 jit_solution(4757595314535918303)
XLA Ops:
  0.0 25.0 %uplink.1 = (bf16[8,128,1024]{2,1,0:T(8,128)(2,1)}, bf16[32,128]{1,0:T(8,128)(2,1)}, f32[32,128]{1,0:T(8,128)}) custom-call(bf16[2,4,2,128,1024]{4,3,2,1,0:T(8,128)(2,1)} %guess_hbm.1, bf16[2,4,2,4,1024]{4,3,2,1,0:T(4,128)(2,1)} %received_hbm.1, f32[1,128]{1,0:T(1,128)} %bitcast.9, f32[1,2]{1,0:T(1,128)} %bitcast.10, f32[2,128]{1,0:T(2,128)} %gain_hbm.1, ...), custom_call_target="tpu_custom_call" | custom-call | tf_op jit(solution)/shard_map/uplink/pallas_call | solution.py:843
  25.0 2.8 %place.1 = f32[32,4,16,128]{3,2,1,0:T(8,128)} custom-call(bf16[32,128]{1,0:T(8,128)(2,1)} %get-tuple-element.8.place_hbm, f32[32,128]{1,0:T(8,128)} %get-tuple-element.9.scale_hbm, bf16[8,128,1024]{2,1,0:T(8,128)(2,1)} %get-tuple-element.10.share_hbm), custom_call_target="tpu_custom_call" | custom-call | tf_op jit(solution)/shard_map/place/pallas_call | solution.py:918
